TPU v7x, 128 devices: a whole 4x4x4 slice. The times are simulated.
128 devices in a mesh: lev: 4 (over z), lat: 4 (over y_hi, core), lon: 8 (over y_lo, x).
Axes of the slice: x: 4, y: 4 (y_hi: 2, y_lo: 2; y = y_hi * 2 + y_lo), z: 4, core: 2. Of those that a mesh axis runs over, the one named last changes fastest.
Arguments:
- latent: bfloat16 [256, 128, 1024], P(None, 'lat', 'lon'), may hold values from -6 to 6
- conv_weight: bfloat16 [16, 128, 9, 256], P('lev'), may hold values from -0.125 to 0.125
- mid_weight: bfloat16 [16, 128, 128], P('lev'), may hold values from -0.5 to 0.5
- out_weight: bfloat16 [16, 48, 128], P('lev'), may hold values from -0.5 to 0.5
- vertical_inner_matrix: bfloat16 [1024, 768], replicated, may hold values from -0.21875 to 0.21875
- vertical_outer_matrix: bfloat16 [768, 1024], replicated, may hold values from -0.1875 to 0.1875
- obs_values: float32 [4, 8, 256, 768], P('lat', 'lon'), may hold values from -6 to 6
- obs_weight: float32 [768], replicated, may hold values from 0.25 to 4
- obs_index: int32 [4, 8, 256], P('lat', 'lon'), may hold values from 0 to 4095
- obs_count: int32 [4, 8], P('lat', 'lon'), may hold values from 64 to 256
Outputs:
- latent_grad: float32 [256, 128, 1024], P('lev', 'lat', 'lon')
Inputs may be any that keep to these rules, and one draw needn't show every extreme that they name: `obs_index`: row-major index of a cell within its tile of 32 x 128 cells; indices may repeat. `obs_count`: slots from this number on hold no observation.
All inputs are finite; a program needn't handle non-finite values.
Results may differ from a plain program's by a relative error of at most 0.007.
Values may be sent and summed in bfloat16 or wider, within the bound.
A program may use at most 192 MiB of HBM per device.

v0:
```python
import functools

import jax
import jax.numpy as jnp
from jax import lax
from jax.experimental import pallas as pl
from jax.experimental.pallas import tpu as pltpu
from jax.sharding import PartitionSpec as P

KAPPA = 0.7978845608028654
CUBIC = 0.044715
F32 = jnp.float32
BF16 = jnp.bfloat16
MESH = pl.DeviceIdType.MESH


def gelu_slope(pre):
    tanh_v = jnp.tanh(KAPPA * (pre + CUBIC * pre * pre * pre))
    half = 0.5 * (1.0 + tanh_v)
    value = pre * half
    slope = half + 0.5 * pre * (1.0 - tanh_v * tanh_v) * (KAPPA + 3.0 * KAPPA * CUBIC * pre * pre)
    return (value, slope)


def dot_nn(x, y):
    return lax.dot_general(x, y, (((1,), (0,)), ((), ())), preferred_element_type=F32)


def dot_nt(x, y):
    return lax.dot_general(x, y, (((1,), (1,)), ((), ())), preferred_element_type=F32)


def iota(shape, dim):
    return lax.broadcasted_iota(jnp.int32, shape, dim)


def loop(count, body, unroll=1):
    def step(i, carry):
        body(i)
        return carry

    lax.fori_loop(0, count, step, 0, unroll=unroll)


def kernel(
    latent_hbm,
    conv_hbm,
    mid_ref,
    out_ref,
    inner_hbm,
    outer_hbm,
    obs_hbm,
    weight_ref,
    index_ref,
    count_ref,
    grad_ref,
    raw,
    wide,
    slab,
    conv,
    inner,
    outer,
    obs,
    pick,
    edge,
    side_pick,
    side_send,
    side,
    north,
    south,
    pre,
    act,
    slope_one,
    slope_two,
    slope_col,
    fields,
    fields_t,
    cast,
    misfit,
    out_pad,
    eye,
    taps,
    taps_in,
    summed,
    up_part,
    mid_part,
    down_part,
    row_send,
    row_in,
    side_out,
    side_in,
    load_sem,
    halo_send,
    halo_recv,
    field_send,
    field_recv,
    taps_send,
    taps_recv,
    back_send,
    back_recv,
):
    lev, lat, lon = lax.axis_index("lev"), lax.axis_index("lat"), lax.axis_index("lon")
    n_lev, n_lat, n_lon = lax.axis_size("lev"), lax.axis_size("lat"), lax.axis_size("lon")
    slots = pick.shape[1]
    cells = pick.shape[2]
    chans = slab.shape[0]
    rows = cells // 128
    groups, hidden = mid_ref.shape[:2]
    levels = out_ref.shape[1]
    own = groups * levels
    portion = chans // n_lev

    loads = [
        pltpu.make_async_copy(src, dst, load_sem.at[n])
        for n, (src, dst) in enumerate(
            ((latent_hbm, raw), (conv_hbm, conv), (inner_hbm, inner), (outer_hbm, outer), (obs_hbm, obs))
        )
    ]
    for load in loads:
        load.start()

    def tile(dlat, dlon):
        return (lev, lax.rem(lat + dlat + n_lat, n_lat), lax.rem(lon + dlon + n_lon, n_lon))

    def peer(d):
        return (lax.rem(lev + d, n_lev), lat, lon)

    around = [(x, y) for x in (-1, 0, 1) for y in (-1, 0, 1) if (x, y) != (0, 0)]
    barrier = pltpu.get_barrier_semaphore()
    for x, y in around:
        pl.semaphore_signal(barrier, inc=1, device_id=tile(x, y), device_id_type=MESH)
    for d in range(1, n_lev):
        pl.semaphore_signal(barrier, inc=1, device_id=peer(d), device_id_type=MESH)

    square = iota((slots, slots), 0) == iota((slots, slots), 1)
    eye[...] = jnp.where(square, 1.0, 0.0).astype(BF16)
    spread = jnp.broadcast_to(index_ref[...].astype(F32), (slots, slots))
    index = jnp.sum(jnp.where(square, spread, 0.0), axis=1, keepdims=True).astype(jnp.int32)
    row = lax.shift_right_logical(index, 7)
    col = lax.bitwise_and(index, 127)
    live = jnp.where(iota((slots, 1), 0) < count_ref[...], 1.0, 0.0)

    j = iota((128, 1), 0)
    last = (rows - 1) * 128
    spot = jnp.where(j < 32, j * 128 + 127, (j - 32) * 128)
    for at, cell in ((64, last + 127), (80, last), (96, 127), (112, 0)):
        spot = jnp.where(j == at, cell, jnp.where(j > at, -1, spot))

    def cast_rows(i):
        part = pl.ds(pl.multiple_of(i * 256, 256), 256)
        wide[part, :] = raw[part, :].astype(F32)

    def slab_row(r):
        slab[:, pl.ds(pl.multiple_of((r + 1) * 128, 128), 128)] = wide[
            pl.ds(r, chans, stride=rows), :
        ].astype(BF16)

    def edge_block(i):
        start = pl.multiple_of(i * 512, 512)
        edge[:, pl.ds(start, 512)] = jnp.where(iota((128, 512), 1) + start == spot, 1.0, 0.0).astype(BF16)

    loop(cells // 512, edge_block)
    loads[0].wait()
    loop(raw.shape[0] // 256, cast_rows)
    loop(rows, slab_row, 2)
    side_send[...] = dot_nt(edge[...], slab[:, 128 : 128 + cells]).astype(BF16)

    pl.semaphore_wait(barrier, len(around) + n_lev - 1)
    halo = [
        (slab.at[:, 128:256], south, (-1, 0)),
        (slab.at[:, cells : cells + 128], north, (1, 0)),
    ]
    sides = [(0, 32, (0, 1)), (32, 32, (0, -1)), (64, 16, (1, 1)), (80, 16, (1, -1)), (96, 16, (-1, 1)), (112, 16, (-1, -1))]
    for first, length, where in sides:
        halo.append((side_send.at[pl.ds(first, length)], side.at[pl.ds(first, length)], where))
    halo = [
        pltpu.make_async_remote_copy(
            src_ref=src,
            dst_ref=dst,
            send_sem=halo_send.at[n],
            recv_sem=halo_recv.at[n],
            device_id=tile(*where),
            device_id_type=MESH,
        )
        for n, (src, dst, where) in enumerate(halo)
    ]
    for copy in halo:
        copy.start()

    for b in range(3):
        there = col + (b - 1)
        target = jnp.where((there >= 0) & (there < 128), index + (b - 1), -1)

        def pick_block(i, b=b, target=target):
            start = pl.multiple_of(i * 256, 256)
            hit = iota((slots, 256), 1) + start == target
            pick[b, :, pl.ds(start, 256)] = jnp.where(hit, 1.0, 0.0).astype(BF16)

        loop(cells // 256, pick_block)

    for a in range(3):
        line = row + (a - 1)
        above = (line < 0) & (lat > 0)
        below = (line >= rows) & (lat < n_lat - 1)
        inside = (line >= 0) & (line < rows)
        for b in (0, 2):
            first, upper, lower = (0, 64, 96) if b == 0 else (32, 80, 112)
            out = (col == 0) if b == 0 else (col == 127)
            target = jnp.where(inside, first + line, jnp.where(above, upper, jnp.where(below, lower, -1)))
            target = jnp.where(out, target, -1)
            side_pick[a * 3 + b] = jnp.where(iota((slots, 128), 1) == target, 1.0, 0.0).astype(BF16)
        side_pick[a * 3 + 1] = jnp.zeros((slots, 128), BF16)

    out_pad[...] = jnp.zeros(out_pad.shape, BF16)
    for g in range(groups):
        part = pl.ds(pl.multiple_of(lev * own + g * levels, 16), levels)
        out_pad[part, g * hidden : (g + 1) * hidden] = out_ref[g]

    for copy in halo:
        copy.wait_recv()
    has_north = jnp.where(lat > 0, 1.0, 0.0)
    has_south = jnp.where(lat < n_lat - 1, 1.0, 0.0)
    slab[:, 0:128] = (north[...].astype(F32) * has_north).astype(BF16)
    slab[:, 128 + cells : 256 + cells] = (south[...].astype(F32) * has_south).astype(BF16)
    loads[1].wait()
    pre[...] = jnp.zeros(pre.shape, F32)

    def tap(t):
        a, b = t // 3, t % 3
        patch = dot_nt(pick[b], slab[:, pl.ds(pl.multiple_of(a * 128, 128), cells)])
        patch = patch + dot_nn(side_pick[t], side[...])
        kernel_t = conv[:, t].reshape(groups * hidden, chans)
        pre[...] += dot_nt(patch.astype(BF16), kernel_t)

    loop(9, tap)

    step = 32

    def gelu_one(i):
        part = pl.ds(pl.multiple_of(i * step, step), step)
        value, slope = gelu_slope(pre[part, :])
        act[part, :] = value.astype(BF16)
        slope_one[part, :] = slope

    def gelu_two(i):
        part = pl.ds(pl.multiple_of(i * step, step), step)
        value, slope = gelu_slope(pre[part, :])
        act[part, :] = value.astype(BF16)
        slope_two[part, :] = slope

    loop(slots // step, gelu_one)
    for g in range(groups):
        part = slice(g * hidden, (g + 1) * hidden)
        pre[:, part] = dot_nt(act[:, part], mid_ref[g])
    loop(slots // step, gelu_two)
    for g in range(groups):
        part = slice(g * hidden, (g + 1) * hidden)
        fields[pl.ds(pl.multiple_of(lev * own + g * levels, 16), levels), :] = dot_nt(
            out_ref[g], act[:, part]
        ).astype(BF16)

    def field_copy(d, source):
        part = pl.ds(pl.multiple_of(source * own, 16), own)
        return pltpu.make_async_remote_copy(
            src_ref=fields.at[part],
            dst_ref=fields.at[part],
            send_sem=field_send.at[d - 1],
            recv_sem=field_recv.at[d - 1],
            device_id=peer(d),
            device_id_type=MESH,
        )

    field_out = [field_copy(d, lev) for d in range(1, n_lev)]
    for copy in field_out:
        copy.start()
    for load in loads[2:]:
        load.wait()
    for d in range(1, n_lev):
        field_copy(d, lax.rem(lev + n_lev - d, n_lev)).wait_recv()

    for i in range(fields.shape[0] // 256):
        part = slice(i * 256, (i + 1) * 256)
        fields_t[:, part] = dot_nt(eye[...], fields[part, :]).astype(BF16)
    misfit[...] = fields_t[...].astype(F32)

    def column(i):
        part = pl.ds(pl.multiple_of(i * 256, 256), 256)
        value, slope = gelu_slope(dot_nt(fields_t[...], inner[part, :]))
        slope_col[:, part] = slope
        misfit[...] += dot_nt(value.astype(BF16), outer[:, part])

    loop(inner.shape[0] // 256, column)
    misfit[...] = (misfit[...] - obs[...]) * live * weight_ref[...]
    cast[...] = misfit[...].astype(BF16)

    def column_back(i):
        part = pl.ds(pl.multiple_of(i * 256, 256), 256)
        grad_act = (dot_nn(cast[...], outer[:, part]) * slope_col[:, part]).astype(BF16)
        misfit[...] += dot_nn(grad_act, inner[part, :])

    loop(inner.shape[0] // 256, column_back)
    grad_fields = misfit[...].astype(BF16)
    act[...] = (dot_nn(grad_fields, out_pad[...]) * slope_two[...]).astype(BF16)
    for g in range(groups):
        part = slice(g * hidden, (g + 1) * hidden)
        slope_one[:, part] = slope_one[:, part] * dot_nn(act[:, part], mid_ref[g])
    act[...] = slope_one[...].astype(BF16)

    def taps_copy(b, d, target):
        return pltpu.make_async_remote_copy(
            src_ref=taps.at[b, target],
            dst_ref=taps_in.at[b, d - 1],
            send_sem=taps_send.at[b, d - 1],
            recv_sem=taps_recv.at[b, d - 1],
            device_id=peer(d),
            device_id_type=MESH,
        )

    taps_out = []
    for b in range(3):

        def back(a, b=b):
            kernel_t = conv[:, a * 3 + b].reshape(groups * hidden, chans)
            part = dot_nn(act[...], kernel_t).astype(BF16)
            part = dot_nt(eye[...], part).astype(BF16)
            for d in range(n_lev):
                taps[b, d, pl.ds(pl.multiple_of(a * portion, 16), portion), :] = part[
                    d * portion : (d + 1) * portion
                ]

        loop(3, back)
        for d in range(1, n_lev):
            copy = taps_copy(b, d, lax.rem(lev + d, n_lev))
            copy.start()
            taps_out.append(copy)

    for b in range(3):
        for d in range(1, n_lev):
            taps_copy(b, d, lax.rem(lev + d, n_lev)).wait_recv()
        total = taps[b, lev].astype(F32)
        for d in range(1, n_lev):
            total = total + taps_in[b, d - 1].astype(F32)
        summed[b] = total.astype(BF16)

    upper = jnp.zeros((portion, 128), F32)
    lower = jnp.zeros((portion, 128), F32)
    beside = jnp.zeros((portion, 128), F32)
    for b in range(3):
        upper = upper + dot_nn(summed[b, 0:portion], pick[b, :, 0:128])
        lower = lower + dot_nn(summed[b, 2 * portion : 3 * portion], pick[b, :, last : last + 128])
        if b != 1:
            for a in range(3):
                beside = beside + dot_nn(summed[b, a * portion : (a + 1) * portion], side_pick[a * 3 + b])
    row_send[0] = (upper * has_north).astype(BF16)
    row_send[1] = (lower * has_south).astype(BF16)
    side_out[...] = beside.astype(BF16)
    back_copies = [(row_send.at[0], row_in.at[0], (-1, 0)), (row_send.at[1], row_in.at[1], (1, 0))]
    back_sides = [(0, -1), (0, 1), (-1, -1), (-1, 1), (1, -1), (1, 1)]
    for n, where in enumerate(back_sides):
        back_copies.append((side_out, side_in.at[n], where))
    back_copies = [
        pltpu.make_async_remote_copy(
            src_ref=src,
            dst_ref=dst,
            send_sem=back_send.at[n],
            recv_sem=back_recv.at[n],
            device_id=tile(*where),
            device_id_type=MESH,
        )
        for n, (src, dst, where) in enumerate(back_copies)
    ]
    for copy in back_copies:
        copy.start()

    def scatter(i):
        start = pl.multiple_of(i * 512, 512)
        part = dot_nn(summed[0], pick[0, :, pl.ds(start, 512)])
        part = part + dot_nn(summed[1], pick[1, :, pl.ds(start, 512)])
        part = part + dot_nn(summed[2], pick[2, :, pl.ds(start, 512)])
        up_part[:, pl.ds(start, 512)] = part[0:portion]
        mid_part[:, pl.ds(start, 512)] = part[portion : 2 * portion]
        down_part[:, pl.ds(pl.multiple_of(start + 128, 128), 512)] = part[2 * portion :]

    loop(cells // 512, scatter)
    for copy in back_copies:
        copy.wait_recv()
    up_part[:, cells : cells + 128] = row_in[0].astype(F32)
    down_part[:, 0:128] = row_in[1].astype(F32)
    lane = iota((portion, 128), 1)
    block = side_in[0].astype(F32)
    for n, start in ((1, 32), (2, 64), (3, 80), (4, 96), (5, 112)):
        block = jnp.where(lane >= start, side_in[n].astype(F32), block)
    block = block.astype(BF16)

    def finish(r):
        here = pl.ds(pl.multiple_of(r * 128, 128), 128)
        below = pl.ds(pl.multiple_of((r + 1) * 128, 128), 128)
        total = up_part[:, below] + mid_part[:, here] + down_part[:, here] + dot_nn(block, edge[:, here])
        grad_ref[pl.ds(r, portion, stride=rows), :] = total

    loop(rows, finish, 2)
    for copy in halo + field_out + taps_out + back_copies:
        copy.wait_send()


def per_device(
    latent,
    conv_weight,
    mid_weight,
    out_weight,
    vertical_inner_matrix,
    vertical_outer_matrix,
    obs_values,
    obs_weight,
    obs_index,
    obs_count,
):
    chans, rows, cols = latent.shape
    groups, hidden = conv_weight.shape[:2]
    slots, channels = obs_values.shape[2:]
    n_lev = lax.axis_size("lev")
    cells = rows * cols
    portion = chans // n_lev
    width = groups * hidden
    column = vertical_inner_matrix.shape[0]
    conv = conv_weight.transpose(0, 2, 1, 3)
    vmem = pltpu.VMEM
    dma = pltpu.SemaphoreType.DMA
    anywhere = pl.BlockSpec(memory_space=pl.ANY)
    near = pl.BlockSpec(memory_space=pltpu.VMEM)
    grad = pl.pallas_call(
        kernel,
        out_shape=jax.ShapeDtypeStruct((portion * rows, cols), F32),
        in_specs=[anywhere, anywhere, near, near, anywhere, anywhere, anywhere, near, near, near],
        out_specs=near,
        scratch_shapes=[
            vmem((chans * rows, cols), BF16),
            vmem((chans * rows, cols), F32),
            vmem((chans, cells + 2 * cols), BF16),
            vmem(conv.shape, BF16),
            vmem(vertical_inner_matrix.shape, BF16),
            vmem(vertical_outer_matrix.shape, BF16),
            vmem((slots, channels), F32),
            vmem((3, slots, cells), BF16),
            vmem((128, cells), BF16),
            vmem((9, slots, 128), BF16),
            vmem((128, chans), BF16),
            vmem((128, chans), BF16),
            vmem((chans, 128), BF16),
            vmem((chans, 128), BF16),
            vmem((slots, width), F32),
            vmem((slots, width), BF16),
            vmem((slots, width), F32),
            vmem((slots, width), F32),
            vmem((slots, column), F32),
            vmem((channels, slots), BF16),
            vmem((slots, channels), BF16),
            vmem((slots, channels), BF16),
            vmem((slots, channels), F32),
            vmem((channels, width), BF16),
            vmem((slots, slots), BF16),
            vmem((3, n_lev, 3 * portion, slots), BF16),
            vmem((3, n_lev - 1, 3 * portion, slots), BF16),
            vmem((3, 3 * portion, slots), BF16),
            vmem((portion, cells + cols), F32),
            vmem((portion, cells), F32),
            vmem((portion, cells + cols), F32),
            vmem((2, portion, cols), BF16),
            vmem((2, portion, cols), BF16),
            vmem((portion, 128), BF16),
            vmem((6, portion, 128), BF16),
            dma((5,)),
            dma((8,)),
            dma((8,)),
            dma((n_lev - 1,)),
            dma((n_lev - 1,)),
            dma((3, n_lev - 1)),
            dma((3, n_lev - 1)),
            dma((8,)),
            dma((8,)),
        ],
        compiler_params=pltpu.CompilerParams(
            collective_id=0, has_side_effects=True, vmem_limit_bytes=50 * 1024 * 1024
        ),
        name="slots_step",
    )(
        latent.reshape(chans * rows, cols),
        conv,
        mid_weight,
        out_weight,
        vertical_inner_matrix,
        vertical_outer_matrix,
        obs_values.reshape(slots, channels),
        obs_weight.reshape(1, channels),
        obs_index.reshape(1, slots),
        obs_count,
    )
    mine = lax.dynamic_slice_in_dim(latent, lax.axis_index("lev") * portion, portion, 0)
    return mine.astype(F32) + grad.reshape(portion, rows, cols)


def solution(mesh):
    return jax.shard_map(
        per_device,
        mesh=mesh,
        in_specs=(
            P(None, "lat", "lon"),
            P("lev", None, None, None),
            P("lev", None, None),
            P("lev", None, None),
            P(),
            P(),
            P("lat", "lon", None, None),
            P(),
            P("lat", "lon", None),
            P("lat", "lon"),
        ),
        out_specs=P("lev", "lat", "lon"),
        check_vma=False,
    )
```

profile of v0, /device:TPU:1, one launch (start us, length us, event | category | flops | bytes accessed | tf_op | source)
XLA Modules:
  0.0 73.3 jit_solution(18401762670605138788)
XLA Ops:
  0.7 0.7 reshape.17.weight_ref
  1.3 0.0 copy-start
  1.3 1.4 %copy-done = bf16[1024,768]{1,0:T(8,128)(2,1)S(1)} copy-done((bf16[1024,768]{1,0:T(8,128)(2,1)S(1)}, bf16[1024,768]{1,0:T(8,128)(2,1)}, u32[]{:S(2)}) %copy-start) | copy-done | bytes 1572888
  2.8 0.0 copy-start.1
  2.8 1.1 %copy-done.1 = f32[1,1,256,768]{3,2,1,0:T(8,128)S(1)} copy-done((f32[1,1,256,768]{3,2,1,0:T(8,128)S(1)}, f32[1,1,256,768]{3,2,1,0:T(8,128)}, u32[]{:S(2)}) %copy-start.1) | copy-done | bytes 786456
  3.9 0.0 copy-start.2
  3.9 0.9 %copy-done.2 = bf16[4,128,128]{2,1,0:T(8,128)(2,1)S(1)} copy-done((bf16[4,128,128]{2,1,0:T(8,128)(2,1)S(1)}, bf16[4,128,128]{2,1,0:T(8,128)(2,1)}, u32[]{:S(2)}) %copy-start.2) | copy-done | bytes 131096
  4.8 0.0 copy-start.3
  4.8 0.8 %copy-done.3 = bf16[4,48,128]{2,1,0:T(8,128)(2,1)S(1)} copy-done((bf16[4,48,128]{2,1,0:T(8,128)(2,1)S(1)}, bf16[4,48,128]{2,1,0:T(8,128)(2,1)}, u32[]{:S(2)}) %copy-start.3) | copy-done | bytes 49176
  5.6 0.0 copy-start.4
  5.6 0.7 copy-done.4
  6.3 64.8 %slots_step.1 = f32[2048,128]{1,0:T(8,128)S(1)} custom-call(bf16[8192,128]{1,0:T(8,128)(2,1)} %bitcast.8, bf16[4,9,128,256]{3,2,1,0:T(8,128)(2,1)} %bitcast.9, bf16[4,128,128]{2,1,0:T(8,128)(2,1)S(1)} %copy-done.2, bf16[4,48,128]{2,1,0:T(8,128)(2,1)S(1)} %copy-done.3, bf16[1024,768]{1,0:T(8,128)(2,1)S(1)} %copy-done, bf16[768,1024]{1,0:T(8,128)(2,1)} %outer_hbm.1, ...), custom_call_target="tpu_custom_call" | custom-call | tf_op jit(solution)/shard_map/slots_step/pallas_call | solution.py:431
  71.1 2.2 %convert_add_fusion = f32[64,32,128]{2,1,0:T(8,128)} fusion(f32[64,32,128]{2,1,0:T(8,128)S(1)} %bitcast.5, bf16[256,32,128]{2,1,0:T(8,128)(2,1)} %param.10, s32[]{:T(128)S(6)} %select_n.3), kind=kLoop, calls=%fused_computation | loop fusion | flops 524288 | bytes 2621444 | tf_op jit(solution)/shard_map/add | solution.py:499
Async XLA Ops:
  1.3 1.4 %copy-start = (bf16[1024,768]{1,0:T(8,128)(2,1)S(1)}, bf16[1024,768]{1,0:T(8,128)(2,1)}, u32[]{:S(2)}) copy-start(bf16[1024,768]{1,0:T(8,128)(2,1)} %inner_hbm.1) | copy-start | bytes 4718596
  2.8 1.1 %copy-start.1 = (f32[1,1,256,768]{3,2,1,0:T(8,128)S(1)}, f32[1,1,256,768]{3,2,1,0:T(8,128)}, u32[]{:S(2)}) copy-start(f32[1,1,256,768]{3,2,1,0:T(8,128)} %param.16) | copy-start | bytes 2359300
  3.9 0.9 %copy-start.2 = (bf16[4,128,128]{2,1,0:T(8,128)(2,1)S(1)}, bf16[4,128,128]{2,1,0:T(8,128)(2,1)}, u32[]{:S(2)}) copy-start(bf16[4,128,128]{2,1,0:T(8,128)(2,1)} %mid_ref.1) | copy-start | bytes 393220
  4.8 0.8 %copy-start.3 = (bf16[4,48,128]{2,1,0:T(8,128)(2,1)S(1)}, bf16[4,48,128]{2,1,0:T(8,128)(2,1)}, u32[]{:S(2)}) copy-start(bf16[4,48,128]{2,1,0:T(8,128)(2,1)} %out_ref.1) | copy-start | bytes 147460
  5.6 0.7 copy-start.4
where the time goes:
time: 73.6 us; the launch traced here: 73.3 us
  Pallas kernels  64.8 us (88%)
  local copies, waits for them, and re-layouts  5.61 us (8%)
  other arithmetic  2.17 us (3%)
    pallas_call x1, Pallas kernels, per_device(): pl.pallas_call(kernel, out_shape=jax.ShapeDtypeStruct((portion * rows, co...  64.8 us
    unnamed x10, local copies, waits for them, and re-layouts  4.92 us
    add x1, other arithmetic, per_device(): return mine.astype(F32) + grad.reshape(portion, rows, cols)  2.17 us

commit v1 on v0

v1 whole, which is shorter than its diff:
```python
import functools

import jax
import jax.numpy as jnp
from jax import lax
from jax.experimental import pallas as pl
from jax.experimental.pallas import tpu as pltpu
from jax.sharding import PartitionSpec as P

KAPPA = 0.7978845608028654
CUBIC = 0.044715
F32 = jnp.float32
BF16 = jnp.bfloat16
MESH = pl.DeviceIdType.MESH


def gelu_slope(pre):
    tanh_v = jnp.tanh(KAPPA * (pre + CUBIC * pre * pre * pre))
    half = 0.5 * (1.0 + tanh_v)
    value = pre * half
    slope = half + 0.5 * pre * (1.0 - tanh_v * tanh_v) * (KAPPA + 3.0 * KAPPA * CUBIC * pre * pre)
    return (value, slope)


def dot_nn(x, y):
    return lax.dot_general(x, y, (((1,), (0,)), ((), ())), preferred_element_type=F32)


def dot_nt(x, y):
    return lax.dot_general(x, y, (((1,), (1,)), ((), ())), preferred_element_type=F32)


def iota(shape, dim):
    return lax.broadcasted_iota(jnp.int32, shape, dim)


def loop(count, body, unroll=1):
    def step(i, carry):
        body(i)
        return carry

    lax.fori_loop(0, count, step, 0, unroll=unroll)


def kernel(
    latent_hbm,
    conv_hbm,
    mid_hbm,
    out_hbm,
    inner_hbm,
    outer_hbm,
    obs_hbm,
    weight_hbm,
    index_hbm,
    count_hbm,
    grad_ref,
    raw,
    conv,
    mid_ref,
    out_ref,
    inner,
    outer,
    obs,
    weight_ref,
    index_ref,
    count_ref,
    index_smem,
    slab,
    table,
    patch,
    pick,
    edge,
    side_pick,
    side_send,
    side,
    row_out,
    north,
    south,
    pre,
    act,
    slope_one,
    slope_two,
    act_col,
    slope_col,
    fields,
    fields_t,
    cast,
    misfit,
    out_pad,
    eye,
    taps,
    relay_in,
    relay_out,
    taps_in,
    up_part,
    mid_part,
    down_part,
    row_send,
    row_in,
    side_out,
    side_in,
    load_sem,
    halo_send,
    halo_recv,
    field_send,
    field_recv,
    relay_send,
    relay_recv,
    taps_send,
    taps_recv,
    back_send,
    back_recv,
):
    lev, lat, lon = lax.axis_index("lev"), lax.axis_index("lat"), lax.axis_index("lon")
    n_lev, n_lat, n_lon = lax.axis_size("lev"), lax.axis_size("lat"), lax.axis_size("lon")
    slots = pick.shape[1]
    cells = pick.shape[2]
    chans = slab.shape[1]
    rows = cells // 128
    groups, hidden = mid_ref.shape[:2]
    levels = out_ref.shape[1]
    own = groups * levels
    portion = chans // n_lev
    pitch = table.shape[0] // (rows + 2)

    pairs = (
        (latent_hbm, raw),
        (index_hbm, index_smem),
        (index_hbm, index_ref),
        (count_hbm, count_ref),
        (conv_hbm, conv),
        (mid_hbm, mid_ref),
        (out_hbm, out_ref),
        (inner_hbm, inner),
        (outer_hbm, outer),
        (obs_hbm, obs),
        (weight_hbm, weight_ref.at[0]),
    )
    loads = [pltpu.make_async_copy(src, dst, load_sem.at[n]) for n, (src, dst) in enumerate(pairs)]
    for load in loads:
        load.start()

    def tile(dlat, dlon):
        return (lev, lax.rem(lat + dlat + n_lat, n_lat), lax.rem(lon + dlon + n_lon, n_lon))

    def peer(d):
        return (lax.rem(lev + d, n_lev), lat, lon)

    around = [(x, y) for x in (-1, 0, 1) for y in (-1, 0, 1) if (x, y) != (0, 0)]
    barrier = pltpu.get_barrier_semaphore()
    for x, y in around:
        pl.semaphore_signal(barrier, inc=1, device_id=tile(x, y), device_id_type=MESH)
    for d in range(1, n_lev):
        pl.semaphore_signal(barrier, inc=1, device_id=peer(d), device_id_type=MESH)

    square = iota((slots, slots), 0) == iota((slots, slots), 1)
    eye[...] = jnp.where(square, 1.0, 0.0).astype(BF16)
    order = iota((slots, 1), 0)
    order = lax.bitwise_and(order, 7) * rows + lax.shift_right_logical(order, 3)
    order = jnp.where(iota((slots, slots), 1) == order, 1.0, 0.0).astype(BF16)
    loads[0].wait()

    def relayout(i):
        start = pl.multiple_of(i * 16 * rows, 16 * rows)
        parts = [
            dot_nn(order, raw[pl.ds(start + h * 8 * rows, 8 * rows), :]).reshape(rows, 8, 128) for h in range(2)
        ]
        slab[:, pl.ds(pl.multiple_of(i * 16, 16), 16), :] = jnp.concatenate(parts, axis=1).astype(BF16)

    loop(chans // 16, relayout, 2)

    def put_row(line, value):
        start = line * pitch + 2
        table[pl.ds(start, 128, stride=2), :] = value[:, 0:128]
        table[pl.ds(start + 1, 128, stride=2), :] = value[:, 128:256]

    def table_row(r):
        put_row(r + 1, dot_nt(eye[0:128, 0:128], slab[r]))

    loop(rows, table_row, 2)

    for n, line in ((0, 0), (1, rows - 1)):
        row_out[n] = dot_nt(eye[0:128, 0:128], slab[line]).astype(BF16)
    for h in range(2):
        part = slice(h * 128, (h + 1) * 128)
        side_send[0:rows, part] = table[pl.ds(pitch + 256 + h, rows, stride=pitch), :]
        side_send[rows : 2 * rows, part] = table[pl.ds(pitch + 2 + h, rows, stride=pitch), :]
        for n, at in enumerate(
            (rows * pitch + 256, rows * pitch + 2, pitch + 256, pitch + 2)
        ):
            first = 2 * rows + 8 * n
            side_send[first : first + 8, part] = jnp.broadcast_to(table[at + h : at + h + 1, :], (8, 128))

    pl.semaphore_wait(barrier, len(around) + n_lev - 1)
    halo = [(row_out.at[0], south, (-1, 0)), (row_out.at[1], north, (1, 0))]
    sides = [(0, 32, (0, 1)), (32, 32, (0, -1)), (64, 8, (1, 1)), (72, 8, (1, -1)), (80, 8, (-1, 1)), (88, 8, (-1, -1))]
    for first, length, where in sides:
        halo.append((side_send.at[pl.ds(first, length)], side.at[pl.ds(first, length)], where))
    halo = [
        pltpu.make_async_remote_copy(
            src_ref=src,
            dst_ref=dst,
            send_sem=halo_send.at[n],
            recv_sem=halo_recv.at[n],
            device_id=tile(*where),
            device_id_type=MESH,
        )
        for n, (src, dst, where) in enumerate(halo)
    ]
    for copy in halo:
        copy.start()

    out_pad[...] = jnp.zeros(out_pad.shape, BF16)
    pre[...] = jnp.zeros(pre.shape, F32)
    for load in loads[1:7]:
        load.wait()
    for g in range(groups):
        part = pl.ds(pl.multiple_of(lev * own + g * levels, 16), levels)
        out_pad[part, g * hidden : (g + 1) * hidden] = out_ref[g]

    for copy in halo:
        copy.wait_recv()
    has_north = jnp.where(lat > 0, 1.0, 0.0)
    has_south = jnp.where(lat < n_lat - 1, 1.0, 0.0)
    put_row(0, north[...].astype(F32) * has_north)
    put_row(rows + 1, south[...].astype(F32) * has_south)
    for h in range(2):
        part = slice(h * 128, (h + 1) * 128)
        table[pl.ds(pitch + h, rows, stride=pitch), :] = side[0:rows, part]
        table[pl.ds(pitch + 258 + h, rows, stride=pitch), :] = side[rows : 2 * rows, part]
        low = (rows + 1) * pitch
        for n, (at, scale) in enumerate(((0, has_north), (258, has_north), (low, has_south), (low + 258, has_south))):
            first = 2 * rows + 8 * n
            table[at + h : at + h + 1, :] = side[first : first + 1, part] * scale

    def slot_patch(k):
        where = index_smem[0, k]
        start = lax.shift_right_logical(where, 7) * pitch + lax.bitwise_and(where, 127) * 2
        for a in range(3):
            patch[pl.ds(pl.multiple_of(k * 24 + a * 8, 8), 8), :] = table[pl.ds(start + a * pitch, 8), :]

    loop(slots, slot_patch, 8)

    def tap(a):
        for b in range(3):
            parts = [patch[pl.ds(a * 8 + b * 2 + h, slots, stride=24), :] for h in range(2)]
            cells_t = jnp.concatenate(parts, axis=1).astype(BF16)
            pre[...] += dot_nt(cells_t, conv[:, a * 3 + b].reshape(groups * hidden, chans))

    loop(3, tap)

    step = 32

    def gelu_one(i):
        part = pl.ds(pl.multiple_of(i * step, step), step)
        value, slope = gelu_slope(pre[part, :])
        act[part, :] = value.astype(BF16)
        slope_one[part, :] = slope

    def gelu_two(i):
        part = pl.ds(pl.multiple_of(i * step, step), step)
        value, slope = gelu_slope(pre[part, :])
        act[part, :] = value.astype(BF16)
        slope_two[part, :] = slope

    loop(slots // step, gelu_one)
    for g in range(groups):
        part = slice(g * hidden, (g + 1) * hidden)
        pre[:, part] = dot_nt(act[:, part], mid_ref[g])
    loop(slots // step, gelu_two)
    for g in range(groups):
        part = slice(g * hidden, (g + 1) * hidden)
        fields[pl.ds(pl.multiple_of(lev * own + g * levels, 16), levels), :] = dot_nt(
            out_ref[g], act[:, part]
        ).astype(BF16)

    def field_copy(d, source):
        part = pl.ds(pl.multiple_of(source * own, 16), own)
        return pltpu.make_async_remote_copy(
            src_ref=fields.at[part],
            dst_ref=fields.at[part],
            send_sem=field_send.at[d - 1],
            recv_sem=field_recv.at[d - 1],
            device_id=peer(d),
            device_id_type=MESH,
        )

    field_out = [field_copy(d, lev) for d in range(1, n_lev)]
    for copy in field_out:
        copy.start()

    spread = jnp.broadcast_to(index_ref[...].astype(F32), (slots, slots))
    index = jnp.sum(jnp.where(square, spread, 0.0), axis=1, keepdims=True).astype(jnp.int32)
    row = lax.shift_right_logical(index, 7)
    col = lax.bitwise_and(index, 127)
    live = jnp.where(iota((slots, 1), 0) < count_ref[...], 1.0, 0.0)
    row_wide = jnp.broadcast_to(row, (slots, 128))
    lane_wide = iota((slots, 128), 1)
    last = (rows - 1) * 128
    for b in range(3):
        cast[:, b * 128 : (b + 1) * 128] = jnp.where(lane_wide == col + (b - 1), 1.0, 0.0).astype(BF16)

    def pick_row(r):
        hit = row_wide == r
        for b in range(3):
            column_b = cast[:, b * 128 : (b + 1) * 128].astype(F32)
            pick[b, :, pl.ds(pl.multiple_of(r * 128, 128), 128)] = jnp.where(hit, column_b, 0.0).astype(BF16)

    loop(rows, pick_row)

    for a in range(3):
        line = row + (a - 1)
        above = (line < 0) & (lat > 0)
        below = (line >= rows) & (lat < n_lat - 1)
        inside = (line >= 0) & (line < rows)
        for n, b in enumerate((0, 2)):
            first, upper, lower = (0, 64, 96) if b == 0 else (32, 80, 112)
            out = (col == 0) if b == 0 else (col == 127)
            target = jnp.where(inside, first + line, jnp.where(above, upper, jnp.where(below, lower, -1)))
            target = jnp.where(out, target, -1)
            side_pick[n * 3 + a] = jnp.where(lane_wide == target, 1.0, 0.0).astype(BF16)

    j = iota((128, 1), 0)
    spot = jnp.where(j < 32, j * 128 + 127, (j - 32) * 128)
    for at, cell in ((64, last + 127), (80, last), (96, 127), (112, 0)):
        spot = jnp.where(j == at, cell, jnp.where(j > at, -1, spot))

    def edge_block(i):
        start = pl.multiple_of(i * 512, 512)
        edge[:, pl.ds(start, 512)] = jnp.where(iota((128, 512), 1) + start == spot, 1.0, 0.0).astype(BF16)

    loop(cells // 512, edge_block)

    for load in loads[7:]:
        load.wait()
    for d in range(1, n_lev):
        field_copy(d, lax.rem(lev + n_lev - d, n_lev)).wait_recv()

    blocks = fields.shape[0] // 256
    for i in range(blocks):
        part = slice(i * 256, (i + 1) * 256)
        fields_t[:, part] = dot_nt(eye[...], fields[part, :]).astype(BF16)

    def column(i):
        part = pl.ds(pl.multiple_of(i * 256, 256), 256)
        value, slope = gelu_slope(dot_nt(fields_t[...], inner[part, :]))
        slope_col[:, part] = slope
        act_col[:, part] = value.astype(BF16)

    loop(inner.shape[0] // 256, column)

    def compare(i):
        part = pl.ds(pl.multiple_of(i * 256, 256), 256)
        forecast = fields_t[:, part].astype(F32) + dot_nt(act_col[...], outer[part, :])
        value = (forecast - obs[:, part]) * live * weight_ref[:, part]
        misfit[:, part] = value
        cast[:, part] = value.astype(BF16)

    loop(blocks, compare)

    def column_back(i):
        part = pl.ds(pl.multiple_of(i * 256, 256), 256)
        act_col[:, part] = (dot_nn(cast[...], outer[:, part]) * slope_col[:, part]).astype(BF16)

    loop(inner.shape[0] // 256, column_back)

    def fields_back(i):
        part = pl.ds(pl.multiple_of(i * 256, 256), 256)
        fields_t[:, part] = (misfit[:, part] + dot_nn(act_col[...], inner[:, part])).astype(BF16)

    loop(blocks, fields_back)
    act[...] = (dot_nn(fields_t[...], out_pad[...]) * slope_two[...]).astype(BF16)
    for g in range(groups):
        part = slice(g * hidden, (g + 1) * hidden)
        slope_one[:, part] = slope_one[:, part] * dot_nn(act[:, part], mid_ref[g])
    act[...] = slope_one[...].astype(BF16)

    above_lev, below_lev, across = lax.rem(lev + 1, n_lev), lax.rem(lev + 3, n_lev), lax.rem(lev + 2, n_lev)
    half = 3 * portion // 2
    low_half, high_half = pl.ds(0, half), pl.ds(half, half)

    def send(src, dst, sems, device):
        return pltpu.make_async_remote_copy(
            src_ref=src,
            dst_ref=dst,
            send_sem=sems[0],
            recv_sem=sems[1],
            device_id=(device, lat, lon),
            device_id_type=MESH,
        )

    def relay_copies(b):
        return [
            send(taps.at[b, across, low_half], relay_in.at[b, 0], (relay_send.at[b, 0], relay_recv.at[b, 0]), above_lev),
            send(taps.at[b, across, high_half], relay_in.at[b, 1], (relay_send.at[b, 1], relay_recv.at[b, 1]), below_lev),
        ]

    def taps_copies(b):
        sources = (
            (relay_out.at[b, 0], above_lev),
            (taps.at[b, above_lev, high_half], above_lev),
            (taps.at[b, below_lev, low_half], below_lev),
            (relay_out.at[b, 1], below_lev),
        )
        return [
            send(src, taps_in.at[b, n], (taps_send.at[b, n], taps_recv.at[b, n]), device)
            for n, (src, device) in enumerate(sources)
        ]

    relays = [relay_copies(b) for b in range(3)]
    shares = [taps_copies(b) for b in range(3)]
    for b in range(3):

        def back(a, b=b):
            kernel_t = conv[:, a * 3 + b].reshape(groups * hidden, chans)
            part = dot_nn(act[...], kernel_t).astype(BF16)
            part = dot_nt(eye[...], part).astype(BF16)
            for d in range(n_lev):
                taps[b, d, pl.ds(pl.multiple_of(a * portion, 16), portion), :] = part[
                    d * portion : (d + 1) * portion
                ]

        loop(3, back)
        for copy in relays[b] + shares[b][1:3]:
            copy.start()
    for b in range(3):
        for copy in relays[b]:
            copy.wait_recv()
        for n, (device, part) in enumerate(((above_lev, low_half), (below_lev, high_half))):
            mine = taps[b, device, part, :].astype(F32)
            relay_out[b, n] = (mine + relay_in[b, n].astype(F32)).astype(BF16)
        shares[b][0].start()
        shares[b][3].start()

    upper = jnp.zeros((portion, 128), F32)
    lower = jnp.zeros((portion, 128), F32)
    beside = jnp.zeros((portion, 128), F32)
    for b in range(3):
        for copy in shares[b]:
            copy.wait_recv()
        halves = []
        for part, first, second in ((low_half, 0, 2), (high_half, 1, 3)):
            total = taps[b, lev, part, :].astype(F32)
            halves.append(total + taps_in[b, first].astype(F32) + taps_in[b, second].astype(F32))
        summed = jnp.concatenate(halves, axis=0).astype(BF16)
        upper = upper + dot_nn(summed[0:portion], pick[b, :, 0:128])
        lower = lower + dot_nn(summed[2 * portion : 3 * portion], pick[b, :, last : last + 128])
        if b != 1:
            for a in range(3):
                beside = beside + dot_nn(summed[a * portion : (a + 1) * portion], side_pick[(b // 2) * 3 + a])
        if b == 2:
            row_send[0] = (upper * has_north).astype(BF16)
            row_send[1] = (lower * has_south).astype(BF16)
            side_out[...] = beside.astype(BF16)
            back_copies = [(row_send.at[0], row_in.at[0], (-1, 0)), (row_send.at[1], row_in.at[1], (1, 0))]
            back_sides = [(0, -1), (0, 1), (-1, -1), (-1, 1), (1, -1), (1, 1)]
            for n, where in enumerate(back_sides):
                back_copies.append((side_out, side_in.at[n], where))
            back_copies = [
                pltpu.make_async_remote_copy(
                    src_ref=src,
                    dst_ref=dst,
                    send_sem=back_send.at[n],
                    recv_sem=back_recv.at[n],
                    device_id=tile(*where),
                    device_id_type=MESH,
                )
                for n, (src, dst, where) in enumerate(back_copies)
            ]
            for copy in back_copies:
                copy.start()

        def scatter(i, b=b, summed=summed):
            here = pl.ds(pl.multiple_of(i * 512, 512), 512)
            after = pl.ds(pl.multiple_of(i * 512 + 128, 128), 512)
            part = dot_nn(summed, pick[b, :, here])
            if b == 0:
                up_part[:, here] = part[0:portion]
                mid_part[:, here] = part[portion : 2 * portion]
                down_part[:, after] = part[2 * portion :]
            else:
                up_part[:, here] += part[0:portion]
                mid_part[:, here] += part[portion : 2 * portion]
                down_part[:, after] += part[2 * portion :]

        loop(cells // 512, scatter)

    for copy in back_copies:
        copy.wait_recv()
    up_part[:, cells : cells + 128] = row_in[0].astype(F32)
    down_part[:, 0:128] = row_in[1].astype(F32)
    lane = iota((portion, 128), 1)
    block = side_in[0].astype(F32)
    for n, start in ((1, 32), (2, 64), (3, 80), (4, 96), (5, 112)):
        block = jnp.where(lane >= start, side_in[n].astype(F32), block)
    block = block.astype(BF16)

    def finish(r):
        here = pl.ds(pl.multiple_of(r * 128, 128), 128)
        below = pl.ds(pl.multiple_of((r + 1) * 128, 128), 128)
        total = up_part[:, below] + mid_part[:, here] + down_part[:, here] + dot_nn(block, edge[:, here])
        grad_ref[pl.ds(r, portion, stride=rows), :] = total

    loop(rows, finish, 2)
    for copy in halo + field_out + sum(relays, []) + sum(shares, []) + back_copies:
        copy.wait_send()


def per_device(
    latent,
    conv_weight,
    mid_weight,
    out_weight,
    vertical_inner_matrix,
    vertical_outer_matrix,
    obs_values,
    obs_weight,
    obs_index,
    obs_count,
):
    chans, rows, cols = latent.shape
    groups, hidden = conv_weight.shape[:2]
    slots, channels = obs_values.shape[2:]
    n_lev = lax.axis_size("lev")
    cells = rows * cols
    portion = chans // n_lev
    width = groups * hidden
    column = vertical_inner_matrix.shape[0]
    conv = conv_weight.transpose(0, 2, 1, 3)
    half = 3 * portion // 2
    vmem = pltpu.VMEM
    dma = pltpu.SemaphoreType.DMA
    grad = pl.pallas_call(
        kernel,
        out_shape=jax.ShapeDtypeStruct((portion * rows, cols), F32),
        in_specs=[pl.BlockSpec(memory_space=pl.ANY)] * 10,
        out_specs=pl.BlockSpec(memory_space=pltpu.VMEM),
        scratch_shapes=[
            vmem((chans * rows, cols), BF16),
            vmem(conv.shape, BF16),
            vmem(mid_weight.shape, BF16),
            vmem(out_weight.shape, BF16),
            vmem(vertical_inner_matrix.shape, BF16),
            vmem(vertical_outer_matrix.shape, BF16),
            vmem((slots, channels), F32),
            vmem((1, channels), F32),
            vmem((1, slots), jnp.int32),
            vmem((1, 1), jnp.int32),
            pltpu.SMEM((1, slots), jnp.int32),
            vmem((rows, chans, cols), BF16),
            vmem(((rows + 2) * 2 * (cols + 8), 128), F32),
            vmem((slots * 24, 128), F32),
            vmem((3, slots, cells), BF16),
            vmem((128, cells), BF16),
            vmem((6, slots, 128), BF16),
            vmem((2 * rows + 32, chans), F32),
            vmem((2 * rows + 32, chans), F32),
            vmem((2, cols, chans), BF16),
            vmem((cols, chans), BF16),
            vmem((cols, chans), BF16),
            vmem((slots, width), F32),
            vmem((slots, width), BF16),
            vmem((slots, width), F32),
            vmem((slots, width), F32),
            vmem((slots, column), BF16),
            vmem((slots, column), F32),
            vmem((channels, slots), BF16),
            vmem((slots, channels), BF16),
            vmem((slots, channels), BF16),
            vmem((slots, channels), F32),
            vmem((channels, width), BF16),
            vmem((slots, slots), BF16),
            vmem((3, n_lev, 3 * portion, slots), BF16),
            vmem((3, 2, half, slots), BF16),
            vmem((3, 2, half, slots), BF16),
            vmem((3, 4, half, slots), BF16),
            vmem((portion, cells + cols), F32),
            vmem((portion, cells), F32),
            vmem((portion, cells + cols), F32),
            vmem((2, portion, cols), BF16),
            vmem((2, portion, cols), BF16),
            vmem((portion, 128), BF16),
            vmem((6, portion, 128), BF16),
            dma((11,)),
            dma((8,)),
            dma((8,)),
            dma((n_lev - 1,)),
            dma((n_lev - 1,)),
            dma((3, 2)),
            dma((3, 2)),
            dma((3, 4)),
            dma((3, 4)),
            dma((8,)),
            dma((8,)),
        ],
        compiler_params=pltpu.CompilerParams(
            collective_id=0, has_side_effects=True, vmem_limit_bytes=60 * 1024 * 1024
        ),
        name="slots_step",
    )(
        latent.reshape(chans * rows, cols),
        conv,
        mid_weight,
        out_weight,
        vertical_inner_matrix,
        vertical_outer_matrix,
        obs_values.reshape(slots, channels),
        obs_weight,
        obs_index.reshape(1, slots),
        obs_count,
    )
    mine = lax.dynamic_slice_in_dim(latent, lax.axis_index("lev") * portion, portion, 0)
    return mine.astype(F32) + grad.reshape(portion, rows, cols)


def solution(mesh):
    return jax.shard_map(
        per_device,
        mesh=mesh,
        in_specs=(
            P(None, "lat", "lon"),
            P("lev", None, None, None),
            P("lev", None, None),
            P("lev", None, None),
            P(),
            P(),
            P("lat", "lon", None, None),
            P(),
            P("lat", "lon", None),
            P("lat", "lon"),
        ),
        out_specs=P("lev", "lat", "lon"),
        check_vma=False,
    )
```

time: 73.6 us -> 59.2 us (0.80)
  Pallas kernels: 64.8 us -> 55.9 us
  local copies, waits for them, and re-layouts: 5.61 us -> 0 us
    pallas_call x1, Pallas kernels: 64.8 us -> 55.9 us  [per_device(): pl.pallas_call(kernel, out_shape=jax.ShapeDtypeStruct((portion * rows, co...]
    unnamed x10 -> x0, local copies, waits for them, and re-layouts: 4.92 us -> none
where the time goes in v1:
time: 59.2 us; the launch traced here: 59.1 us
  Pallas kernels  55.9 us (94%)
  other arithmetic  2.49 us (4%)
  between operations  0.66 us (1%)
    pallas_call x1, Pallas kernels, per_device(): pl.pallas_call(kernel, out_shape=jax.ShapeDtypeStruct((portion * rows, co...  55.9 us
    add x1, other arithmetic, per_device(): return mine.astype(F32) + grad.reshape(portion, rows, cols)  2.49 us

profile of v1, /device:TPU:1, one launch (start us, length us, event | category | flops | bytes accessed | tf_op | source)
XLA Modules:
  0.0 59.1 jit_solution(11129650532849565246)
XLA Ops:
  0.7 55.9 %slots_step.1 = f32[2048,128]{1,0:T(8,128)} custom-call(bf16[8192,128]{1,0:T(8,128)(2,1)} %bitcast.6, bf16[4,9,128,256]{3,2,1,0:T(8,128)(2,1)} %bitcast.7, bf16[4,128,128]{2,1,0:T(8,128)(2,1)} %mid_hbm.1, bf16[4,48,128]{2,1,0:T(8,128)(2,1)} %out_hbm.1, bf16[1024,768]{1,0:T(8,128)(2,1)} %inner_hbm.1, bf16[768,1024]{1,0:T(8,128)(2,1)} %outer_hbm.1, ...), custom_call_target="tpu_custom_call" | custom-call | tf_op jit(solution)/shard_map/slots_step/pallas_call | solution.py:533
  56.6 2.5 %convert_add_fusion = f32[64,32,128]{2,1,0:T(8,128)} fusion(f32[64,32,128]{2,1,0:T(8,128)} %bitcast.5, bf16[256,32,128]{2,1,0:T(8,128)(2,1)} %param.10, s32[]{:T(128)S(6)} %select_n.3), kind=kLoop, calls=%fused_computation | loop fusion | flops 524288 | bytes 2621444 | tf_op jit(solution)/shard_map/add | solution.py:613

commit v2 on v1

--- a/solution.py
+++ b/solution.py
@@ -137,7 +137,7 @@
         (weight_hbm, weight_ref.at[0]),
     )
     loads = [pltpu.make_async_copy(src, dst, load_sem.at[n]) for n, (src, dst) in enumerate(pairs)]
-    for load in loads:
+    for load in loads[:4]:
         load.start()
 
     def tile(dlat, dlon):
@@ -159,6 +159,8 @@
     order = lax.bitwise_and(order, 7) * rows + lax.shift_right_logical(order, 3)
     order = jnp.where(iota((slots, slots), 1) == order, 1.0, 0.0).astype(BF16)
     loads[0].wait()
+    for load in loads[4:]:
+        load.start()
 
     def relayout(i):
         start = pl.multiple_of(i * 16 * rows, 16 * rows)
@@ -247,7 +249,7 @@
             cells_t = jnp.concatenate(parts, axis=1).astype(BF16)
             pre[...] += dot_nt(cells_t, conv[:, a * 3 + b].reshape(groups * hidden, chans))
 
-    loop(3, tap)
+    loop(3, tap, 3)
 
     step = 32
 
@@ -330,6 +332,8 @@
         edge[:, pl.ds(start, 512)] = jnp.where(iota((128, 512), 1) + start == spot, 1.0, 0.0).astype(BF16)
 
     loop(cells // 512, edge_block)
+    up_part[:, cells : cells + 128] = jnp.zeros((portion, 128), F32)
+    down_part[:, 0:128] = jnp.zeros((portion, 128), F32)
 
     for load in loads[7:]:
         load.wait()
@@ -347,7 +351,7 @@
         slope_col[:, part] = slope
         act_col[:, part] = value.astype(BF16)
 
-    loop(inner.shape[0] // 256, column)
+    loop(inner.shape[0] // 256, column, 4)
 
     def compare(i):
         part = pl.ds(pl.multiple_of(i * 256, 256), 256)
@@ -356,19 +360,19 @@
         misfit[:, part] = value
         cast[:, part] = value.astype(BF16)
 
-    loop(blocks, compare)
+    loop(blocks, compare, 3)
 
     def column_back(i):
         part = pl.ds(pl.multiple_of(i * 256, 256), 256)
         act_col[:, part] = (dot_nn(cast[...], outer[:, part]) * slope_col[:, part]).astype(BF16)
 
-    loop(inner.shape[0] // 256, column_back)
+    loop(inner.shape[0] // 256, column_back, 4)
 
     def fields_back(i):
         part = pl.ds(pl.multiple_of(i * 256, 256), 256)
         fields_t[:, part] = (misfit[:, part] + dot_nn(act_col[...], inner[:, part])).astype(BF16)
 
-    loop(blocks, fields_back)
+    loop(blocks, fields_back, 3)
     act[...] = (dot_nn(fields_t[...], out_pad[...]) * slope_two[...]).astype(BF16)
     for g in range(groups):
         part = slice(g * hidden, (g + 1) * hidden)
@@ -420,9 +424,12 @@
                     d * portion : (d + 1) * portion
                 ]
 
-        loop(3, back)
-        for copy in relays[b] + shares[b][1:3]:
+        loop(3, back, 3)
+        for copy in relays[b]:
             copy.start()
+    for b in range(3):
+        shares[b][1].start()
+        shares[b][2].start()
     for b in range(3):
         for copy in relays[b]:
             copy.wait_recv()
@@ -483,25 +490,31 @@
                 mid_part[:, here] += part[portion : 2 * portion]
                 down_part[:, after] += part[2 * portion :]
 
-        loop(cells // 512, scatter)
-
+        loop(cells // 512, scatter, 2)
+
+    def finish(r):
+        here = pl.ds(pl.multiple_of(r * 128, 128), 128)
+        below = pl.ds(pl.multiple_of((r + 1) * 128, 128), 128)
+        grad_ref[pl.ds(r, portion, stride=rows), :] = up_part[:, below] + mid_part[:, here] + down_part[:, here]
+
+    loop(rows, finish, 4)
     for copy in back_copies:
         copy.wait_recv()
-    up_part[:, cells : cells + 128] = row_in[0].astype(F32)
-    down_part[:, 0:128] = row_in[1].astype(F32)
     lane = iota((portion, 128), 1)
     block = side_in[0].astype(F32)
     for n, start in ((1, 32), (2, 64), (3, 80), (4, 96), (5, 112)):
         block = jnp.where(lane >= start, side_in[n].astype(F32), block)
     block = block.astype(BF16)
 
-    def finish(r):
-        here = pl.ds(pl.multiple_of(r * 128, 128), 128)
-        below = pl.ds(pl.multiple_of((r + 1) * 128, 128), 128)
-        total = up_part[:, below] + mid_part[:, here] + down_part[:, here] + dot_nn(block, edge[:, here])
-        grad_ref[pl.ds(r, portion, stride=rows), :] = total
-
-    loop(rows, finish, 2)
+    for n, line in ((0, rows - 1), (1, 0)):
+        grad_ref[pl.ds(line, portion, stride=rows), :] += row_in[n].astype(F32)
+
+    def patch_edges(i):
+        part = dot_nn(block, edge[:, pl.ds(pl.multiple_of(i * 1024, 1024), 1024)])
+        for n in range(8):
+            grad_ref[pl.ds(i * 8 + n, portion, stride=rows), :] += part[:, n * 128 : (n + 1) * 128]
+
+    loop(rows // 8, patch_edges, 4)
     for copy in halo + field_out + sum(relays, []) + sum(shares, []) + back_copies:
         copy.wait_send()
 

time: 59.2 us -> 52.8 us (0.89)
  Pallas kernels: 55.9 us -> 49.5 us
    pallas_call x1, Pallas kernels: 55.9 us -> 49.5 us  [per_device(): pl.pallas_call(kernel, out_shape=jax.ShapeDtypeStruct((portion * rows, co...]
where the time goes in v2:
time: 52.8 us; the launch traced here: 52.7 us
  Pallas kernels  49.5 us (94%)
  other arithmetic  2.49 us (5%)
  between operations  0.66 us (1%)
    pallas_call x1, Pallas kernels, per_device(): pl.pallas_call(kernel, out_shape=jax.ShapeDtypeStruct((portion * rows, co...  49.5 us
    add x1, other arithmetic, per_device(): return mine.astype(F32) + grad.reshape(portion, rows, cols)  2.49 us

profile of v2, /device:TPU:1, one launch (start us, length us, event | category | flops | bytes accessed | tf_op | source)
XLA Modules:
  0.0 52.7 jit_solution(9706762446455025747)
XLA Ops:
  0.7 49.5 %slots_step.1 = f32[2048,128]{1,0:T(8,128)} custom-call(bf16[8192,128]{1,0:T(8,128)(2,1)} %bitcast.6, bf16[4,9,128,256]{3,2,1,0:T(8,128)(2,1)} %bitcast.7, bf16[4,128,128]{2,1,0:T(8,128)(2,1)} %mid_hbm.1, bf16[4,48,128]{2,1,0:T(8,128)(2,1)} %out_hbm.1, bf16[1024,768]{1,0:T(8,128)(2,1)} %inner_hbm.1, bf16[768,1024]{1,0:T(8,128)(2,1)} %outer_hbm.1, ...), custom_call_target="tpu_custom_call" | custom-call | tf_op jit(solution)/shard_map/slots_step/pallas_call | solution.py:546
  50.2 2.5 %convert_add_fusion = f32[64,32,128]{2,1,0:T(8,128)} fusion(f32[64,32,128]{2,1,0:T(8,128)} %bitcast.5, bf16[256,32,128]{2,1,0:T(8,128)(2,1)} %param.10, s32[]{:T(128)S(6)} %select_n.3), kind=kLoop, calls=%fused_computation | loop fusion | flops 524288 | bytes 2621444 | tf_op jit(solution)/shard_map/add | solution.py:626

commit v3 on v2

--- a/solution.py
+++ b/solution.py
@@ -68,6 +68,7 @@
     slab,
     table,
     patch,
+    patches,
     pick,
     edge,
     side_pick,
@@ -92,6 +93,7 @@
     relay_in,
     relay_out,
     taps_in,
+    summed,
     up_part,
     mid_part,
     down_part,
@@ -99,6 +101,7 @@
     row_in,
     side_out,
     side_in,
+    first_sem,
     load_sem,
     halo_send,
     halo_recv,
@@ -124,7 +127,6 @@
     pitch = table.shape[0] // (rows + 2)
 
     pairs = (
-        (latent_hbm, raw),
         (index_hbm, index_smem),
         (index_hbm, index_ref),
         (count_hbm, count_ref),
@@ -137,7 +139,12 @@
         (weight_hbm, weight_ref.at[0]),
     )
     loads = [pltpu.make_async_copy(src, dst, load_sem.at[n]) for n, (src, dst) in enumerate(pairs)]
-    for load in loads[:4]:
+    pieces = 4
+    first_loads = []
+    for n in range(pieces):
+        part = pl.ds(n * (raw.shape[0] // pieces), raw.shape[0] // pieces)
+        first_loads.append(pltpu.make_async_copy(latent_hbm.at[part], raw.at[part], first_sem.at[n]))
+    for load in first_loads + loads[:3]:
         load.start()
 
     def tile(dlat, dlon):
@@ -158,18 +165,21 @@
     order = iota((slots, 1), 0)
     order = lax.bitwise_and(order, 7) * rows + lax.shift_right_logical(order, 3)
     order = jnp.where(iota((slots, slots), 1) == order, 1.0, 0.0).astype(BF16)
-    loads[0].wait()
-    for load in loads[4:]:
-        load.start()
 
     def relayout(i):
-        start = pl.multiple_of(i * 16 * rows, 16 * rows)
+        start = i * 16 * rows
         parts = [
             dot_nn(order, raw[pl.ds(start + h * 8 * rows, 8 * rows), :]).reshape(rows, 8, 128) for h in range(2)
         ]
-        slab[:, pl.ds(pl.multiple_of(i * 16, 16), 16), :] = jnp.concatenate(parts, axis=1).astype(BF16)
-
-    loop(chans // 16, relayout, 2)
+        slab[:, pl.ds(i * 16, 16), :] = jnp.concatenate(parts, axis=1).astype(BF16)
+
+    for n, load in enumerate(first_loads):
+        load.wait()
+        if n == pieces - 1:
+            for later in loads[3:]:
+                later.start()
+        for i in range(chans // 16 // pieces):
+            relayout(n * (chans // 16 // pieces) + i)
 
     def put_row(line, value):
         start = line * pitch + 2
@@ -179,7 +189,7 @@
     def table_row(r):
         put_row(r + 1, dot_nt(eye[0:128, 0:128], slab[r]))
 
-    loop(rows, table_row, 2)
+    loop(rows, table_row, rows)
 
     for n, line in ((0, 0), (1, rows - 1)):
         row_out[n] = dot_nt(eye[0:128, 0:128], slab[line]).astype(BF16)
@@ -213,8 +223,7 @@
         copy.start()
 
     out_pad[...] = jnp.zeros(out_pad.shape, BF16)
-    pre[...] = jnp.zeros(pre.shape, F32)
-    for load in loads[1:7]:
+    for load in loads[:6]:
         load.wait()
     for g in range(groups):
         part = pl.ds(pl.multiple_of(lev * own + g * levels, 16), levels)
@@ -243,53 +252,61 @@
 
     loop(slots, slot_patch, 8)
 
-    def tap(a):
-        for b in range(3):
-            parts = [patch[pl.ds(a * 8 + b * 2 + h, slots, stride=24), :] for h in range(2)]
-            cells_t = jnp.concatenate(parts, axis=1).astype(BF16)
-            pre[...] += dot_nt(cells_t, conv[:, a * 3 + b].reshape(groups * hidden, chans))
-
-    loop(3, tap, 3)
-
     step = 32
-
-    def gelu_one(i):
-        part = pl.ds(pl.multiple_of(i * step, step), step)
-        value, slope = gelu_slope(pre[part, :])
-        act[part, :] = value.astype(BF16)
-        slope_one[part, :] = slope
-
-    def gelu_two(i):
-        part = pl.ds(pl.multiple_of(i * step, step), step)
-        value, slope = gelu_slope(pre[part, :])
-        act[part, :] = value.astype(BF16)
-        slope_two[part, :] = slope
-
-    loop(slots // step, gelu_one)
-    for g in range(groups):
-        part = slice(g * hidden, (g + 1) * hidden)
-        pre[:, part] = dot_nt(act[:, part], mid_ref[g])
-    loop(slots // step, gelu_two)
-    for g in range(groups):
-        part = slice(g * hidden, (g + 1) * hidden)
-        fields[pl.ds(pl.multiple_of(lev * own + g * levels, 16), levels), :] = dot_nt(
-            out_ref[g], act[:, part]
-        ).astype(BF16)
-
-    def field_copy(d, source):
-        part = pl.ds(pl.multiple_of(source * own, 16), own)
+    sets = 2
+    per_set = groups // sets
+
+    def field_copy(p, d, source):
+        part = pl.ds(pl.multiple_of(source * own + p * (own // sets), 16), own // sets)
         return pltpu.make_async_remote_copy(
             src_ref=fields.at[part],
             dst_ref=fields.at[part],
-            send_sem=field_send.at[d - 1],
-            recv_sem=field_recv.at[d - 1],
+            send_sem=field_send.at[p, d - 1],
+            recv_sem=field_recv.at[p, d - 1],
             device_id=peer(d),
             device_id_type=MESH,
         )
 
-    field_out = [field_copy(d, lev) for d in range(1, n_lev)]
-    for copy in field_out:
-        copy.start()
+    field_out = []
+    for p in range(sets):
+        span = slice(p * per_set * hidden, (p + 1) * per_set * hidden)
+        first = p * per_set
+        total = None
+        for t in range(9):
+            if p == 0:
+                parts = [patch[pl.ds((t // 3) * 8 + (t % 3) * 2 + h, slots, stride=24), :] for h in range(2)]
+                patches[t] = jnp.concatenate(parts, axis=1).astype(BF16)
+            kernel_t = conv[first : first + per_set, t].reshape(per_set * hidden, chans)
+            part = dot_nt(patches[t], kernel_t)
+            total = part if total is None else total + part
+        pre[:, span] = total
+
+        def gelu_one(i, span=span):
+            part = pl.ds(pl.multiple_of(i * step, step), step)
+            value, slope = gelu_slope(pre[part, span])
+            act[part, span] = value.astype(BF16)
+            slope_one[part, span] = slope
+
+        def gelu_two(i, span=span):
+            part = pl.ds(pl.multiple_of(i * step, step), step)
+            value, slope = gelu_slope(pre[part, span])
+            act[part, span] = value.astype(BF16)
+            slope_two[part, span] = slope
+
+        loop(slots // step, gelu_one, 4)
+        for g in range(first, first + per_set):
+            part = slice(g * hidden, (g + 1) * hidden)
+            pre[:, part] = dot_nt(act[:, part], mid_ref[g])
+        loop(slots // step, gelu_two, 4)
+        for g in range(first, first + per_set):
+            part = slice(g * hidden, (g + 1) * hidden)
+            fields[pl.ds(pl.multiple_of(lev * own + g * levels, 16), levels), :] = dot_nt(
+                out_ref[g], act[:, part]
+            ).astype(BF16)
+        for d in range(1, n_lev):
+            copy = field_copy(p, d, lev)
+            copy.start()
+            field_out.append(copy)
 
     spread = jnp.broadcast_to(index_ref[...].astype(F32), (slots, slots))
     index = jnp.sum(jnp.where(square, spread, 0.0), axis=1, keepdims=True).astype(jnp.int32)
@@ -335,10 +352,11 @@
     up_part[:, cells : cells + 128] = jnp.zeros((portion, 128), F32)
     down_part[:, 0:128] = jnp.zeros((portion, 128), F32)
 
-    for load in loads[7:]:
+    for load in loads[6:]:
         load.wait()
-    for d in range(1, n_lev):
-        field_copy(d, lax.rem(lev + n_lev - d, n_lev)).wait_recv()
+    for p in range(sets):
+        for d in range(1, n_lev):
+            field_copy(p, d, lax.rem(lev + n_lev - d, n_lev)).wait_recv()
 
     blocks = fields.shape[0] // 256
     for i in range(blocks):
@@ -449,12 +467,13 @@
         for part, first, second in ((low_half, 0, 2), (high_half, 1, 3)):
             total = taps[b, lev, part, :].astype(F32)
             halves.append(total + taps_in[b, first].astype(F32) + taps_in[b, second].astype(F32))
-        summed = jnp.concatenate(halves, axis=0).astype(BF16)
-        upper = upper + dot_nn(summed[0:portion], pick[b, :, 0:128])
-        lower = lower + dot_nn(summed[2 * portion : 3 * portion], pick[b, :, last : last + 128])
+        summed_b = jnp.concatenate(halves, axis=0).astype(BF16)
+        summed[b] = summed_b
+        upper = upper + dot_nn(summed_b[0:portion], pick[b, :, 0:128])
+        lower = lower + dot_nn(summed_b[2 * portion : 3 * portion], pick[b, :, last : last + 128])
         if b != 1:
             for a in range(3):
-                beside = beside + dot_nn(summed[a * portion : (a + 1) * portion], side_pick[(b // 2) * 3 + a])
+                beside = beside + dot_nn(summed_b[a * portion : (a + 1) * portion], side_pick[(b // 2) * 3 + a])
         if b == 2:
             row_send[0] = (upper * has_north).astype(BF16)
             row_send[1] = (lower * has_south).astype(BF16)
@@ -477,20 +496,17 @@
             for copy in back_copies:
                 copy.start()
 
-        def scatter(i, b=b, summed=summed):
-            here = pl.ds(pl.multiple_of(i * 512, 512), 512)
-            after = pl.ds(pl.multiple_of(i * 512 + 128, 128), 512)
-            part = dot_nn(summed, pick[b, :, here])
-            if b == 0:
-                up_part[:, here] = part[0:portion]
-                mid_part[:, here] = part[portion : 2 * portion]
-                down_part[:, after] = part[2 * portion :]
-            else:
-                up_part[:, here] += part[0:portion]
-                mid_part[:, here] += part[portion : 2 * portion]
-                down_part[:, after] += part[2 * portion :]
-
-        loop(cells // 512, scatter, 2)
+    def scatter(i):
+        here = pl.ds(pl.multiple_of(i * 512, 512), 512)
+        after = pl.ds(pl.multiple_of(i * 512 + 128, 128), 512)
+        part = dot_nn(summed[0], pick[0, :, here])
+        part = part + dot_nn(summed[1], pick[1, :, here])
+        part = part + dot_nn(summed[2], pick[2, :, here])
+        up_part[:, here] = part[0:portion]
+        mid_part[:, here] = part[portion : 2 * portion]
+        down_part[:, after] = part[2 * portion :]
+
+    loop(cells // 512, scatter, 2)
 
     def finish(r):
         here = pl.ds(pl.multiple_of(r * 128, 128), 128)
@@ -543,6 +559,18 @@
     half = 3 * portion // 2
     vmem = pltpu.VMEM
     dma = pltpu.SemaphoreType.DMA
+    operands = [
+        latent.reshape(chans * rows, cols),
+        conv,
+        mid_weight,
+        out_weight,
+        vertical_inner_matrix,
+        vertical_outer_matrix,
+        obs_values.reshape(slots, channels),
+        obs_weight,
+        obs_index.reshape(1, slots),
+    ]
+    operands = [pltpu.with_memory_space_constraint(x, pltpu.HBM) for x in operands]
     grad = pl.pallas_call(
         kernel,
         out_shape=jax.ShapeDtypeStruct((portion * rows, cols), F32),
@@ -563,6 +591,7 @@
             vmem((rows, chans, cols), BF16),
             vmem(((rows + 2) * 2 * (cols + 8), 128), F32),
             vmem((slots * 24, 128), F32),
+            vmem((9, slots, chans), BF16),
             vmem((3, slots, cells), BF16),
             vmem((128, cells), BF16),
             vmem((6, slots, 128), BF16),
@@ -587,6 +616,7 @@
             vmem((3, 2, half, slots), BF16),
             vmem((3, 2, half, slots), BF16),
             vmem((3, 4, half, slots), BF16),
+            vmem((3, 3 * portion, slots), BF16),
             vmem((portion, cells + cols), F32),
             vmem((portion, cells), F32),
             vmem((portion, cells + cols), F32),
@@ -594,11 +624,12 @@
             vmem((2, portion, cols), BF16),
             vmem((portion, 128), BF16),
             vmem((6, portion, 128), BF16),
-            dma((11,)),
+            dma((4,)),
+            dma((10,)),
             dma((8,)),
             dma((8,)),
-            dma((n_lev - 1,)),
-            dma((n_lev - 1,)),
+            dma((2, n_lev - 1)),
+            dma((2, n_lev - 1)),
             dma((3, 2)),
             dma((3, 2)),
             dma((3, 4)),
@@ -607,21 +638,10 @@
             dma((8,)),
         ],
         compiler_params=pltpu.CompilerParams(
-            collective_id=0, has_side_effects=True, vmem_limit_bytes=60 * 1024 * 1024
+            collective_id=0, has_side_effects=True, vmem_limit_bytes=50 * 1024 * 1024
         ),
         name="slots_step",
-    )(
-        latent.reshape(chans * rows, cols),
-        conv,
-        mid_weight,
-        out_weight,
-        vertical_inner_matrix,
-        vertical_outer_matrix,
-        obs_values.reshape(slots, channels),
-        obs_weight,
-        obs_index.reshape(1, slots),
-        obs_count,
-    )
+    )(*operands, obs_count)
     mine = lax.dynamic_slice_in_dim(latent, lax.axis_index("lev") * portion, portion, 0)
     return mine.astype(F32) + grad.reshape(portion, rows, cols)
 

time: 52.8 us -> 46.8 us (0.89)
  Pallas kernels: 49.5 us -> 43.7 us
    pallas_call x1, Pallas kernels: 49.5 us -> 43.7 us  [per_device(): pl.pallas_call(kernel, out_shape=jax.ShapeDtypeStruct((portion * rows, co...]
where the time goes in v3:
time: 46.8 us; the launch traced here: 46.6 us
  Pallas kernels  43.7 us (93%)
  other arithmetic  2.18 us (5%)
  between operations  0.66 us (1%)
    pallas_call x1, Pallas kernels, per_device(): pl.pallas_call(kernel, out_shape=jax.ShapeDtypeStruct((portion * rows, co...  43.7 us
    add x1, other arithmetic, per_device(): return mine.astype(F32) + grad.reshape(portion, rows, cols)  2.18 us

profile of v3, /device:TPU:1, one launch (start us, length us, event | category | flops | bytes accessed | tf_op | source)
XLA Modules:
  0.0 46.6 jit_solution(10431434702703358950)
XLA Ops:
  0.7 43.7 %slots_step.1 = f32[2048,128]{1,0:T(8,128)S(1)} custom-call(bf16[8192,128]{1,0:T(8,128)(2,1)} %bitcast.6, bf16[4,9,128,256]{3,2,1,0:T(8,128)(2,1)} %bitcast.7, bf16[4,128,128]{2,1,0:T(8,128)(2,1)} %mid_hbm.1, bf16[4,48,128]{2,1,0:T(8,128)(2,1)} %out_hbm.1, bf16[1024,768]{1,0:T(8,128)(2,1)} %inner_hbm.1, bf16[768,1024]{1,0:T(8,128)(2,1)} %outer_hbm.1, ...), custom_call_target="tpu_custom_call" | custom-call | tf_op jit(solution)/shard_map/slots_step/pallas_call | solution.py:574
  44.4 2.2 %convert_add_fusion = f32[64,32,128]{2,1,0:T(8,128)} fusion(f32[64,32,128]{2,1,0:T(8,128)S(1)} %bitcast.5, bf16[256,32,128]{2,1,0:T(8,128)(2,1)} %param.10, s32[]{:T(128)S(6)} %select_n.3), kind=kLoop, calls=%fused_computation | loop fusion | flops 524288 | bytes 2621444 | tf_op jit(solution)/shard_map/add | solution.py:646

commit v4 on v3

--- a/solution.py
+++ b/solution.py
@@ -101,6 +101,8 @@
     row_in,
     side_out,
     side_in,
+    strips,
+    strips_in,
     first_sem,
     load_sem,
     halo_send,
@@ -113,6 +115,8 @@
     taps_recv,
     back_send,
     back_recv,
+    strip_send,
+    strip_recv,
 ):
     lev, lat, lon = lax.axis_index("lev"), lax.axis_index("lat"), lax.axis_index("lon")
     n_lev, n_lat, n_lon = lax.axis_size("lev"), lax.axis_size("lat"), lax.axis_size("lon")
@@ -303,7 +307,7 @@
             fields[pl.ds(pl.multiple_of(lev * own + g * levels, 16), levels), :] = dot_nt(
                 out_ref[g], act[:, part]
             ).astype(BF16)
-        for d in range(1, n_lev):
+        for d in (1, 3) if p == 0 else (2, 1, 3):
             copy = field_copy(p, d, lev)
             copy.start()
             field_out.append(copy)
@@ -349,14 +353,25 @@
         edge[:, pl.ds(start, 512)] = jnp.where(iota((128, 512), 1) + start == spot, 1.0, 0.0).astype(BF16)
 
     loop(cells // 512, edge_block)
-    up_part[:, cells : cells + 128] = jnp.zeros((portion, 128), F32)
-    down_part[:, 0:128] = jnp.zeros((portion, 128), F32)
-
+
+    field_copy(0, 3, lax.rem(lev + 1, n_lev)).wait_recv()
+    part = pl.ds(pl.multiple_of(lax.rem(lev + 1, n_lev) * own, 16), own // sets)
+    onward = pltpu.make_async_remote_copy(
+        src_ref=fields.at[part],
+        dst_ref=fields.at[part],
+        send_sem=field_send.at[0, 1],
+        recv_sem=field_recv.at[0, 1],
+        device_id=peer(3),
+        device_id_type=MESH,
+    )
+    onward.start()
+    field_out.append(onward)
     for load in loads[6:]:
         load.wait()
     for p in range(sets):
         for d in range(1, n_lev):
-            field_copy(p, d, lax.rem(lev + n_lev - d, n_lev)).wait_recv()
+            if (p, d) != (0, 3):
+                field_copy(p, d, lax.rem(lev + n_lev - d, n_lev)).wait_recv()
 
     blocks = fields.shape[0] // 256
     for i in range(blocks):
@@ -448,6 +463,38 @@
     for b in range(3):
         shares[b][1].start()
         shares[b][2].start()
+
+    upper = jnp.zeros((chans, 128), F32)
+    lower = jnp.zeros((chans, 128), F32)
+    beside = jnp.zeros((chans, 128), F32)
+    for b in range(3):
+        tap_b = [taps[b, :, a * portion : (a + 1) * portion, :].reshape(chans, slots) for a in range(3)]
+        upper = upper + dot_nn(tap_b[0], pick[b, :, 0:128])
+        lower = lower + dot_nn(tap_b[2], pick[b, :, last : last + 128])
+        if b != 1:
+            for a in range(3):
+                beside = beside + dot_nn(tap_b[a], side_pick[(b // 2) * 3 + a])
+    row_send[0] = (upper * has_north).astype(BF16)
+    row_send[1] = (lower * has_south).astype(BF16)
+    side_out[...] = dot_nt(eye[0:128, 0:128], beside.astype(BF16)).astype(BF16)
+    back_copies = [(row_send.at[0], row_in.at[0], (-1, 0)), (row_send.at[1], row_in.at[1], (1, 0))]
+    back_sides = [(0, 32, (0, -1)), (32, 32, (0, 1)), (64, 16, (-1, -1)), (80, 16, (-1, 1)), (96, 16, (1, -1)), (112, 16, (1, 1))]
+    for first, length, where in back_sides:
+        back_copies.append((side_out.at[pl.ds(first, length)], side_in.at[pl.ds(first, length)], where))
+    back_copies = [
+        pltpu.make_async_remote_copy(
+            src_ref=src,
+            dst_ref=dst,
+            send_sem=back_send.at[n],
+            recv_sem=back_recv.at[n],
+            device_id=tile(*where),
+            device_id_type=MESH,
+        )
+        for n, (src, dst, where) in enumerate(back_copies)
+    ]
+    for copy in back_copies:
+        copy.start()
+
     for b in range(3):
         for copy in relays[b]:
             copy.wait_recv()
@@ -457,9 +504,18 @@
         shares[b][0].start()
         shares[b][3].start()
 
-    upper = jnp.zeros((portion, 128), F32)
-    lower = jnp.zeros((portion, 128), F32)
-    beside = jnp.zeros((portion, 128), F32)
+    for copy in back_copies:
+        copy.wait_recv()
+    for n in range(2):
+        strips[:, :, n * 128 : (n + 1) * 128] = row_in[n].reshape(n_lev, portion, 128)
+    strips[:, :, 256:384] = dot_nt(eye[...], side_in[...]).astype(BF16).reshape(n_lev, portion, 128)
+    strip_copies = [
+        send(strips.at[lax.rem(lev + d, n_lev)], strips_in.at[d - 1], (strip_send.at[d - 1], strip_recv.at[d - 1]), lax.rem(lev + d, n_lev))
+        for d in (2, 1, 3)
+    ]
+    for copy in strip_copies:
+        copy.start()
+
     for b in range(3):
         for copy in shares[b]:
             copy.wait_recv()
@@ -467,71 +523,42 @@
         for part, first, second in ((low_half, 0, 2), (high_half, 1, 3)):
             total = taps[b, lev, part, :].astype(F32)
             halves.append(total + taps_in[b, first].astype(F32) + taps_in[b, second].astype(F32))
-        summed_b = jnp.concatenate(halves, axis=0).astype(BF16)
-        summed[b] = summed_b
-        upper = upper + dot_nn(summed_b[0:portion], pick[b, :, 0:128])
-        lower = lower + dot_nn(summed_b[2 * portion : 3 * portion], pick[b, :, last : last + 128])
-        if b != 1:
-            for a in range(3):
-                beside = beside + dot_nn(summed_b[a * portion : (a + 1) * portion], side_pick[(b // 2) * 3 + a])
-        if b == 2:
-            row_send[0] = (upper * has_north).astype(BF16)
-            row_send[1] = (lower * has_south).astype(BF16)
-            side_out[...] = beside.astype(BF16)
-            back_copies = [(row_send.at[0], row_in.at[0], (-1, 0)), (row_send.at[1], row_in.at[1], (1, 0))]
-            back_sides = [(0, -1), (0, 1), (-1, -1), (-1, 1), (1, -1), (1, 1)]
-            for n, where in enumerate(back_sides):
-                back_copies.append((side_out, side_in.at[n], where))
-            back_copies = [
-                pltpu.make_async_remote_copy(
-                    src_ref=src,
-                    dst_ref=dst,
-                    send_sem=back_send.at[n],
-                    recv_sem=back_recv.at[n],
-                    device_id=tile(*where),
-                    device_id_type=MESH,
-                )
-                for n, (src, dst, where) in enumerate(back_copies)
-            ]
-            for copy in back_copies:
-                copy.start()
-
-    def scatter(i):
-        here = pl.ds(pl.multiple_of(i * 512, 512), 512)
-        after = pl.ds(pl.multiple_of(i * 512 + 128, 128), 512)
-        part = dot_nn(summed[0], pick[0, :, here])
-        part = part + dot_nn(summed[1], pick[1, :, here])
-        part = part + dot_nn(summed[2], pick[2, :, here])
-        up_part[:, here] = part[0:portion]
-        mid_part[:, here] = part[portion : 2 * portion]
-        down_part[:, after] = part[2 * portion :]
-
-    loop(cells // 512, scatter, 2)
-
-    def finish(r):
-        here = pl.ds(pl.multiple_of(r * 128, 128), 128)
-        below = pl.ds(pl.multiple_of((r + 1) * 128, 128), 128)
-        grad_ref[pl.ds(r, portion, stride=rows), :] = up_part[:, below] + mid_part[:, here] + down_part[:, here]
-
-    loop(rows, finish, 4)
-    for copy in back_copies:
+        summed[b] = jnp.concatenate(halves, axis=0).astype(BF16)
+
+        def scatter(i, b=b):
+            here = pl.ds(pl.multiple_of(i * 512, 512), 512)
+            after = pl.ds(pl.multiple_of(i * 512 + 128, 128), 512)
+            part = dot_nn(summed[b], pick[b, :, here])
+            if b == 0:
+                up_part[:, here] = part[0:portion]
+                mid_part[:, here] = part[portion : 2 * portion]
+                down_part[:, after] = part[2 * portion :]
+            else:
+                up_part[:, here] += part[0:portion]
+                mid_part[:, here] += part[portion : 2 * portion]
+                down_part[:, after] += part[2 * portion :]
+
+        loop(cells // 512, scatter, 4)
+
+    for copy in strip_copies:
         copy.wait_recv()
-    lane = iota((portion, 128), 1)
-    block = side_in[0].astype(F32)
-    for n, start in ((1, 32), (2, 64), (3, 80), (4, 96), (5, 112)):
-        block = jnp.where(lane >= start, side_in[n].astype(F32), block)
-    block = block.astype(BF16)
-
-    for n, line in ((0, rows - 1), (1, 0)):
-        grad_ref[pl.ds(line, portion, stride=rows), :] += row_in[n].astype(F32)
-
-    def patch_edges(i):
-        part = dot_nn(block, edge[:, pl.ds(pl.multiple_of(i * 1024, 1024), 1024)])
+    strip = strips[lev].astype(F32)
+    for d in range(1, n_lev):
+        strip = strip + strips_in[d - 1].astype(F32)
+    up_part[:, cells : cells + 128] = strip[:, 0:128]
+    down_part[:, 0:128] = strip[:, 128:256]
+    block = strip[:, 256:384].astype(BF16)
+
+    def finish(i):
+        start = i * 1024
+        here = pl.ds(pl.multiple_of(start, 1024), 1024)
+        below = pl.ds(pl.multiple_of(start + 128, 128), 1024)
+        total = up_part[:, below] + mid_part[:, here] + down_part[:, here] + dot_nn(block, edge[:, here])
         for n in range(8):
-            grad_ref[pl.ds(i * 8 + n, portion, stride=rows), :] += part[:, n * 128 : (n + 1) * 128]
-
-    loop(rows // 8, patch_edges, 4)
-    for copy in halo + field_out + sum(relays, []) + sum(shares, []) + back_copies:
+            grad_ref[pl.ds(i * 8 + n, portion, stride=rows), :] = total[:, n * 128 : (n + 1) * 128]
+
+    loop(rows // 8, finish, 4)
+    for copy in halo + field_out + sum(relays, []) + sum(shares, []) + back_copies + strip_copies:
         copy.wait_send()
 
 
@@ -620,10 +647,12 @@
             vmem((portion, cells + cols), F32),
             vmem((portion, cells), F32),
             vmem((portion, cells + cols), F32),
-            vmem((2, portion, cols), BF16),
-            vmem((2, portion, cols), BF16),
-            vmem((portion, 128), BF16),
-            vmem((6, portion, 128), BF16),
+            vmem((2, chans, cols), BF16),
+            vmem((2, chans, cols), BF16),
+            vmem((128, chans), BF16),
+            vmem((128, chans), BF16),
+            vmem((n_lev, portion, 3 * cols), BF16),
+            vmem((n_lev - 1, portion, 3 * cols), BF16),
             dma((4,)),
             dma((10,)),
             dma((8,)),
@@ -636,6 +665,8 @@
             dma((3, 4)),
             dma((8,)),
             dma((8,)),
+            dma((n_lev - 1,)),
+            dma((n_lev - 1,)),
         ],
         compiler_params=pltpu.CompilerParams(
             collective_id=0, has_side_effects=True, vmem_limit_bytes=50 * 1024 * 1024

time: 46.8 us -> 45.1 us (0.964)
  Pallas kernels: 43.7 us -> 42.1 us
    pallas_call x1, Pallas kernels: 43.7 us -> 42.1 us  [per_device(): pl.pallas_call(kernel, out_shape=jax.ShapeDtypeStruct((portion * rows, co...]
where the time goes in v4:
time: 45.1 us; the launch traced here: 44.9 us
  Pallas kernels  42.1 us (93%)
  other arithmetic  2.18 us (5%)
  between operations  0.66 us (1%)
    pallas_call x1, Pallas kernels, per_device(): pl.pallas_call(kernel, out_shape=jax.ShapeDtypeStruct((portion * rows, co...  42.1 us
    add x1, other arithmetic, per_device(): return mine.astype(F32) + grad.reshape(portion, rows, cols)  2.18 us

profile of v4, /device:TPU:1, one launch (start us, length us, event | category | flops | bytes accessed | tf_op | source)
XLA Modules:
  0.0 44.9 jit_solution(7528758238064168482)
XLA Ops:
  0.7 42.1 %slots_step.1 = f32[2048,128]{1,0:T(8,128)S(1)} custom-call(bf16[8192,128]{1,0:T(8,128)(2,1)} %bitcast.6, bf16[4,9,128,256]{3,2,1,0:T(8,128)(2,1)} %bitcast.7, bf16[4,128,128]{2,1,0:T(8,128)(2,1)} %mid_hbm.1, bf16[4,48,128]{2,1,0:T(8,128)(2,1)} %out_hbm.1, bf16[1024,768]{1,0:T(8,128)(2,1)} %inner_hbm.1, bf16[768,1024]{1,0:T(8,128)(2,1)} %outer_hbm.1, ...), custom_call_target="tpu_custom_call" | custom-call | tf_op jit(solution)/shard_map/slots_step/pallas_call | solution.py:601
  42.8 2.2 %convert_add_fusion = f32[64,32,128]{2,1,0:T(8,128)} fusion(f32[64,32,128]{2,1,0:T(8,128)S(1)} %bitcast.5, bf16[256,32,128]{2,1,0:T(8,128)(2,1)} %param.10, s32[]{:T(128)S(6)} %select_n.3), kind=kLoop, calls=%fused_computation | loop fusion | flops 524288 | bytes 2621444 | tf_op jit(solution)/shard_map/add | solution.py:677

commit v5 on v4

--- a/solution.py
+++ b/solution.py
@@ -69,6 +69,7 @@
     table,
     patch,
     patches,
+    conv_t,
     pick,
     edge,
     side_pick,
@@ -366,6 +367,11 @@
     )
     onward.start()
     field_out.append(onward)
+
+    def turn(t):
+        conv_t[t] = dot_nt(eye[...], conv[:, t].reshape(groups * hidden, chans)).astype(BF16)
+
+    loop(9, turn, 3)
     for load in loads[6:]:
         load.wait()
     for p in range(sets):
@@ -449,9 +455,7 @@
     for b in range(3):
 
         def back(a, b=b):
-            kernel_t = conv[:, a * 3 + b].reshape(groups * hidden, chans)
-            part = dot_nn(act[...], kernel_t).astype(BF16)
-            part = dot_nt(eye[...], part).astype(BF16)
+            part = dot_nt(conv_t[a * 3 + b], act[...]).astype(BF16)
             for d in range(n_lev):
                 taps[b, d, pl.ds(pl.multiple_of(a * portion, 16), portion), :] = part[
                     d * portion : (d + 1) * portion
@@ -619,6 +623,7 @@
             vmem(((rows + 2) * 2 * (cols + 8), 128), F32),
             vmem((slots * 24, 128), F32),
             vmem((9, slots, chans), BF16),
+            vmem((9, chans, width), BF16),
             vmem((3, slots, cells), BF16),
             vmem((128, cells), BF16),
             vmem((6, slots, 128), BF16),

time: 45.1 us -> 44.4 us (0.984)
  Pallas kernels: 42.1 us -> 41 us
    pallas_call x1, Pallas kernels: 42.1 us -> 41 us  [per_device(): pl.pallas_call(kernel, out_shape=jax.ShapeDtypeStruct((portion * rows, co...]
where the time goes in v5:
time: 44.4 us; the launch traced here: 43.9 us
  Pallas kernels  41 us (92%)
  other arithmetic  2.18 us (5%)
  between operations  0.66 us (1%)
    pallas_call x1, Pallas kernels, per_device(): pl.pallas_call(kernel, out_shape=jax.ShapeDtypeStruct((portion * rows, co...  41 us
    add x1, other arithmetic, per_device(): return mine.astype(F32) + grad.reshape(portion, rows, cols)  2.18 us

profile of v5, /device:TPU:1, one launch (start us, length us, event | category | flops | bytes accessed | tf_op | source)
XLA Modules:
  0.0 43.9 jit_solution(16826214003290531449)
XLA Ops:
  0.7 41.0 %slots_step.1 = f32[2048,128]{1,0:T(8,128)S(1)} custom-call(bf16[8192,128]{1,0:T(8,128)(2,1)} %bitcast.6, bf16[4,9,128,256]{3,2,1,0:T(8,128)(2,1)} %bitcast.7, bf16[4,128,128]{2,1,0:T(8,128)(2,1)} %mid_hbm.1, bf16[4,48,128]{2,1,0:T(8,128)(2,1)} %out_hbm.1, bf16[1024,768]{1,0:T(8,128)(2,1)} %inner_hbm.1, bf16[768,1024]{1,0:T(8,128)(2,1)} %outer_hbm.1, ...), custom_call_target="tpu_custom_call" | custom-call | tf_op jit(solution)/shard_map/slots_step/pallas_call | solution.py:605
  41.7 2.2 %convert_add_fusion = f32[64,32,128]{2,1,0:T(8,128)} fusion(f32[64,32,128]{2,1,0:T(8,128)S(1)} %bitcast.5, bf16[256,32,128]{2,1,0:T(8,128)(2,1)} %param.10, s32[]{:T(128)S(6)} %select_n.3), kind=kLoop, calls=%fused_computation | loop fusion | flops 524288 | bytes 2621444 | tf_op jit(solution)/shard_map/add | solution.py:682

commit v6 on v5

--- a/solution.py
+++ b/solution.py
@@ -255,7 +255,7 @@
         for a in range(3):
             patch[pl.ds(pl.multiple_of(k * 24 + a * 8, 8), 8), :] = table[pl.ds(start + a * pitch, 8), :]
 
-    loop(slots, slot_patch, 8)
+    loop(slots, slot_patch, 32)
 
     step = 32
     sets = 2
@@ -298,11 +298,11 @@
             act[part, span] = value.astype(BF16)
             slope_two[part, span] = slope
 
-        loop(slots // step, gelu_one, 4)
+        loop(slots // step, gelu_one, 8)
         for g in range(first, first + per_set):
             part = slice(g * hidden, (g + 1) * hidden)
             pre[:, part] = dot_nt(act[:, part], mid_ref[g])
-        loop(slots // step, gelu_two, 4)
+        loop(slots // step, gelu_two, 8)
         for g in range(first, first + per_set):
             part = slice(g * hidden, (g + 1) * hidden)
             fields[pl.ds(pl.multiple_of(lev * own + g * levels, 16), levels), :] = dot_nt(
@@ -542,7 +542,7 @@
                 mid_part[:, here] += part[portion : 2 * portion]
                 down_part[:, after] += part[2 * portion :]
 
-        loop(cells // 512, scatter, 4)
+        loop(cells // 512, scatter, 8)
 
     for copy in strip_copies:
         copy.wait_recv()
@@ -559,7 +559,8 @@
         below = pl.ds(pl.multiple_of(start + 128, 128), 1024)
         total = up_part[:, below] + mid_part[:, here] + down_part[:, here] + dot_nn(block, edge[:, here])
         for n in range(8):
-            grad_ref[pl.ds(i * 8 + n, portion, stride=rows), :] = total[:, n * 128 : (n + 1) * 128]
+            mine = slab[i * 8 + n, pl.ds(pl.multiple_of(lev * portion, 16), portion), :].astype(F32)
+            grad_ref[pl.ds(i * 8 + n, portion, stride=rows), :] = mine + total[:, n * 128 : (n + 1) * 128]
 
     loop(rows // 8, finish, 4)
     for copy in halo + field_out + sum(relays, []) + sum(shares, []) + back_copies + strip_copies:
@@ -678,8 +679,7 @@
         ),
         name="slots_step",
     )(*operands, obs_count)
-    mine = lax.dynamic_slice_in_dim(latent, lax.axis_index("lev") * portion, portion, 0)
-    return mine.astype(F32) + grad.reshape(portion, rows, cols)
+    return grad.reshape(portion, rows, cols)
 
 
 def solution(mesh):

time: 44.4 us -> 42.6 us (0.959); the launches traced: 43.9 us -> 42.5 us
  other arithmetic: 2.18 us -> 0 us
  local copies, waits for them, and re-layouts: 0 us -> 0.97 us
    add x1 -> x0, other arithmetic: 2.18 us -> none  [per_device(): return mine.astype(F32) + grad.reshape(portion, rows, cols)]
    unnamed x0 -> x1, local copies, waits for them, and re-layouts: none -> 0.97 us
where the time goes in v6:
time: 42.6 us; the launch traced here: 42.5 us
  Pallas kernels  40.9 us (96%)
  local copies, waits for them, and re-layouts  0.97 us (2%)
  between operations  0.66 us (2%)
    pallas_call x1, Pallas kernels, per_device(): pl.pallas_call(kernel, out_shape=jax.ShapeDtypeStruct((portion * rows, co...  40.9 us
    unnamed x1, local copies, waits for them, and re-layouts  0.97 us

profile of v6, /device:TPU:1, one launch (start us, length us, event | category | flops | bytes accessed | tf_op | source)
XLA Modules:
  0.0 42.5 jit_solution(11773750577741757250)
XLA Ops:
  0.7 40.9 %slots_step.1 = f32[2048,128]{1,0:T(8,128)S(1)} custom-call(bf16[8192,128]{1,0:T(8,128)(2,1)} %bitcast.7, bf16[4,9,128,256]{3,2,1,0:T(8,128)(2,1)} %bitcast.6, bf16[4,128,128]{2,1,0:T(8,128)(2,1)} %mid_hbm.1, bf16[4,48,128]{2,1,0:T(8,128)(2,1)} %out_hbm.1, bf16[1024,768]{1,0:T(8,128)(2,1)} %inner_hbm.1, bf16[768,1024]{1,0:T(8,128)(2,1)} %outer_hbm.1, ...), custom_call_target="tpu_custom_call" | custom-call | tf_op jit(solution)/shard_map/slots_step/pallas_call | solution.py:606
  41.5 1.0 %copy.13 = f32[64,32,128]{2,1,0:T(8,128)} copy(f32[64,32,128]{2,1,0:T(8,128)S(1)} %bitcast.5) | data formatting | bytes 2097152

commit v7 on v6

--- a/solution.py
+++ b/solution.py
@@ -15,10 +15,10 @@
 
 
 def gelu_slope(pre):
-    tanh_v = jnp.tanh(KAPPA * (pre + CUBIC * pre * pre * pre))
-    half = 0.5 * (1.0 + tanh_v)
+    square = pre * pre
+    half = 0.5 + 0.5 * jnp.tanh(pre * (KAPPA + KAPPA * CUBIC * square))
     value = pre * half
-    slope = half + 0.5 * pre * (1.0 - tanh_v * tanh_v) * (KAPPA + 3.0 * KAPPA * CUBIC * pre * pre)
+    slope = half + value * (1.0 - half) * (2.0 * KAPPA + 6.0 * KAPPA * CUBIC * square)
     return (value, slope)
 
 
@@ -255,9 +255,9 @@
         for a in range(3):
             patch[pl.ds(pl.multiple_of(k * 24 + a * 8, 8), 8), :] = table[pl.ds(start + a * pitch, 8), :]
 
-    loop(slots, slot_patch, 32)
-
-    step = 32
+    loop(slots, slot_patch, 64)
+
+    step = 64
     sets = 2
     per_set = groups // sets
 
@@ -298,11 +298,11 @@
             act[part, span] = value.astype(BF16)
             slope_two[part, span] = slope
 
-        loop(slots // step, gelu_one, 8)
+        loop(slots // step, gelu_one, 4)
         for g in range(first, first + per_set):
             part = slice(g * hidden, (g + 1) * hidden)
             pre[:, part] = dot_nt(act[:, part], mid_ref[g])
-        loop(slots // step, gelu_two, 8)
+        loop(slots // step, gelu_two, 4)
         for g in range(first, first + per_set):
             part = slice(g * hidden, (g + 1) * hidden)
             fields[pl.ds(pl.multiple_of(lev * own + g * levels, 16), levels), :] = dot_nt(
@@ -464,9 +464,6 @@
         loop(3, back, 3)
         for copy in relays[b]:
             copy.start()
-    for b in range(3):
-        shares[b][1].start()
-        shares[b][2].start()
 
     upper = jnp.zeros((chans, 128), F32)
     lower = jnp.zeros((chans, 128), F32)
@@ -498,15 +495,16 @@
     ]
     for copy in back_copies:
         copy.start()
-
     for b in range(3):
-        for copy in relays[b]:
-            copy.wait_recv()
+        shares[b][1].start()
+        shares[b][2].start()
+
+    for b in range(3):
         for n, (device, part) in enumerate(((above_lev, low_half), (below_lev, high_half))):
+            relays[b][n].wait_recv()
             mine = taps[b, device, part, :].astype(F32)
             relay_out[b, n] = (mine + relay_in[b, n].astype(F32)).astype(BF16)
-        shares[b][0].start()
-        shares[b][3].start()
+            shares[b][3 * n].start()
 
     for copy in back_copies:
         copy.wait_recv()

time: 42.6 us -> 42.5 us (level)
  no operation moved by 1% of the time
where the time goes in v7:
time: 42.5 us; the launch traced here: 42.4 us
  Pallas kernels  40.8 us (96%)
  local copies, waits for them, and re-layouts  0.97 us (2%)
  between operations  0.66 us (2%)
    pallas_call x1, Pallas kernels, per_device(): pl.pallas_call(kernel, out_shape=jax.ShapeDtypeStruct((portion * rows, co...  40.8 us
    unnamed x1, local copies, waits for them, and re-layouts  0.97 us

profile of v7, /device:TPU:1, one launch (start us, length us, event | category | flops | bytes accessed | tf_op | source)
XLA Modules:
  0.0 42.4 jit_solution(3896557542331563736)
XLA Ops:
  0.7 40.8 %slots_step.1 = f32[2048,128]{1,0:T(8,128)S(1)} custom-call(bf16[8192,128]{1,0:T(8,128)(2,1)} %bitcast.7, bf16[4,9,128,256]{3,2,1,0:T(8,128)(2,1)} %bitcast.6, bf16[4,128,128]{2,1,0:T(8,128)(2,1)} %mid_hbm.1, bf16[4,48,128]{2,1,0:T(8,128)(2,1)} %out_hbm.1, bf16[1024,768]{1,0:T(8,128)(2,1)} %inner_hbm.1, bf16[768,1024]{1,0:T(8,128)(2,1)} %outer_hbm.1, ...), custom_call_target="tpu_custom_call" | custom-call | tf_op jit(solution)/shard_map/slots_step/pallas_call | solution.py:604
  41.4 1.0 %copy.13 = f32[64,32,128]{2,1,0:T(8,128)} copy(f32[64,32,128]{2,1,0:T(8,128)S(1)} %bitcast.5) | data formatting | bytes 2097152
